TPU v7x, 32 devices: a whole 2x2x4 slice. The times are simulated.
32 devices in a mesh: tx: 4 (over x, core), py: 2 (over y), pz: 4 (over z).
Axes of the slice: x: 2, y: 2, z: 4, core: 2. Of those that a mesh axis runs over, the one named last changes fastest.
Arguments:
- fields: float32 [16, 2, 128, 128, 128], P('tx', None, 'py', 'pz'), may hold values from 0.5 to 1.5
- sources: float32 [16, 2, 128, 128, 128], P('tx', None, 'py', 'pz'), may hold values from -12 to 12
- green: float32 [2, 128, 128, 128], P(None, 'pz', 'py'), may hold values from -6 to 6
Outputs:
- contrast_fine: float32 [2, 256, 256, 256], P(None, 'py', 'pz')
- scattered: float32 [4, 2, 256, 256, 256], P('tx', None, 'py', 'pz')
All inputs are finite; a program needn't handle non-finite values.
Results may differ from a plain program's by a relative error of at most 0.00014.
Values sent between devices are 32-bit elements; how exact they have to be, the bound alone decides.
A program may use at most 192 MiB of HBM per device.

v0:
```python
import math

import jax
import jax.numpy as jnp
from jax import lax
from jax.sharding import PartitionSpec as P

COARSE = 128
FINE = 256


def fourier_matrix(out_index, in_index, period, exponent_sign, weight):
    phases = out_index[:, None] * in_index[None, :] % period
    angles = exponent_sign * 2.0 * math.pi / period * phases.astype(jnp.float32)
    cosine = weight * jnp.cos(angles)
    sine_part = weight * jnp.sin(angles)
    return jnp.stack([jnp.stack([cosine, -sine_part], 1), jnp.stack([sine_part, cosine], 1)], 0)


def local_step(values, matrix):
    return jnp.einsum("fcxyl,dkcl->fdyxk", values, matrix, precision=lax.Precision.HIGHEST)


def remote_step(values, matrix):
    return jnp.einsum("fclxy,dkcl->fdxyk", values, matrix, precision=lax.Precision.HIGHEST)


def turn_depth(values, matrix):

    def finish(received):
        return remote_step(received, matrix)

    return finish(lax.all_to_all(values, "pz", split_axis=4, concat_axis=2, tiled=True))


def turn_height(values, matrix):

    def finish(received):
        return remote_step(received, matrix)

    return finish(lax.all_to_all(values, "py", split_axis=4, concat_axis=2, tiled=True))


def forward_pass(values, matrix):
    return turn_height(turn_depth(local_step(values, matrix), matrix), matrix)


def inverse_pass(values, matrix):
    return turn_depth(turn_height(local_step(values, matrix), matrix), matrix)


def complex_product(first_factor, second_factor):
    real_part = first_factor[0] * second_factor[0] - first_factor[1] * second_factor[1]
    imag_part = first_factor[0] * second_factor[1] + first_factor[1] * second_factor[0]
    return jnp.stack([real_part, imag_part])


def on_device(fields, sources, green):
    coarse_index = jnp.arange(COARSE, dtype=jnp.int32)
    fine_index = jnp.arange(FINE, dtype=jnp.int32)
    signed_coarse = jnp.where(coarse_index < COARSE // 2, coarse_index, coarse_index - COARSE)
    unit_coarse = jnp.ones((COARSE, 1), jnp.float32)
    unit_fine = jnp.ones((FINE, 1), jnp.float32)
    coarse_forward = fourier_matrix(coarse_index, coarse_index, COARSE, -1.0, unit_coarse)
    padded_inverse = fourier_matrix(fine_index, signed_coarse, FINE, 1.0, unit_fine / COARSE)
    field_real = fields[:, 0]
    field_imag = fields[:, 1]
    source_real = sources[:, 0]
    source_imag = sources[:, 1]
    numer_real = jnp.sum(source_real * field_real + source_imag * field_imag, axis=0)
    numer_imag = jnp.sum(source_imag * field_real - source_real * field_imag, axis=0)
    denominator = jnp.sum(field_real * field_real + field_imag * field_imag, axis=0)
    numer_real, numer_imag, denominator = lax.psum((numer_real, numer_imag, denominator), "tx")
    contrast = jnp.stack([numer_real / denominator, numer_imag / denominator])[None]
    source_first = sources[0:1]
    contrast_fine = inverse_pass(forward_pass(contrast, coarse_forward), padded_inverse)[0]
    spectrum = forward_pass(source_first, coarse_forward)
    weighted = complex_product(spectrum[0], green)[None]
    domain_field = inverse_pass(weighted, padded_inverse)[0]
    scattered = complex_product(contrast_fine, domain_field)[None]
    return (contrast_fine, scattered)


def solution(mesh):
    placed = (
        P("tx", None, "py", "pz", None),
        P("tx", None, "py", "pz", None),
        P(None, "pz", "py", None),
    )
    return jax.shard_map(
        on_device,
        mesh=mesh,
        in_specs=placed,
        out_specs=(P(None, "py", "pz", None), P("tx", None, "py", "pz", None)),
        check_vma=False,
    )
```

profile of v0, /device:TPU:0, one launch (start us, length us, event | category | flops | bytes accessed | tf_op | source)
XLA Modules:
  0.0 861.9 jit_solution(6920128943470967341)
XLA Ops:
  24.4 6.3 all-to-all-start.4
  31.3 7.3 add_reduce_fusion.1
  43.4 70.1 %all-reduce.3.cloned.1.call-done = (f32[64,32,128]{2,0,1:T(8,128)}, f32[64,32,128]{2,0,1:T(8,128)}, f32[64,32,128]{2,0,1:T(8,128)}) async-done(((f32[64,32,128]{2,0,1:T(8,128)}, f32[64,32,128]{2,0,1:T(8,128)}, f32[64,32,128]{2,0,1:T(8,128)}), (f32[64,32,128]{2,0,1:T(8,128)}, f32[64,32,128]{2,0,1:T(8,128)}, f32[64,32,128]{2,0,1:T(8,128)})) %all-reduce.3.cloned.1.call-update) | async-done | bytes 3145744 | tf_op jit(solution)/shard_map/psum | solution.py:73
  132.9 7.7 reduce.6
  169.6 10.8 %all-to-all-done = f32[4,1,131072]{2,1,0:T(1,128)} async-done(((f32[4,1,131072]{2,1,0:T(1,128)}), f32[4,1,131072]{2,1,0:T(1,128)}, u32[]{:S(2)}, u32[]{:S(2)}) %all-to-all-start) | async-done | bytes 2097184 | tf_op jit(solution)/shard_map/all_to_all | solution.py:33
  185.2 7.7 reduce.3
  227.5 8.3 reduce.7
  240.2 7.4 copy.95
  259.8 9.1 %copy.60 = f32[1,2,64,32,256]{2,3,1,0,4:T(8,128)} copy(f32[1,2,64,32,256]{4,2,3,1,0:T(8,128)} %convolution_bitcast_fusion.3) | data formatting | bytes 8388608 | tf_op jit(solution)/shard_map/fcxyl,dkcl->fdyxk/transpose | solution.py:21
  268.9 8.7 %reshape.417 = f32[2,1,524288]{2,1,0:T(1,128)} reshape(f32[256,1,2,32,64]{4,3,2,1,0:T(8,128)} %bitcast.220) | data formatting | bytes 8388608
  283.2 8.1 reduce.4
  295.6 7.4 copy.96
  314.6 9.1 %copy.48 = f32[1,2,64,32,256]{2,3,1,0,4:T(8,128)} copy(f32[1,2,64,32,256]{4,2,3,1,0:T(8,128)} %convolution_bitcast_fusion.4) | data formatting | bytes 8388608 | tf_op jit(solution)/shard_map/fcxyl,dkcl->fdyxk/transpose | solution.py:21
  323.7 8.7 %reshape.411 = f32[2,1,524288]{2,1,0:T(1,128)} reshape(f32[256,1,2,32,64]{4,3,2,1,0:T(8,128)} %bitcast.221) | data formatting | bytes 8388608
  338.0 16.7 %reduce.8 = f32[2,524288]{1,0:T(2,128)} reduce(f32[2,1,524288]{2,1,0:T(1,128)} %all-to-all-done.6, f32[]{:T(128)} %broadcast.301), dimensions={1}, to_apply=%all_to_all.106.reduce_sub_computation | reduce | bytes 8388612 | tf_op jit(solution)/shard_map/all_to_all | solution.py:41
  354.8 10.1 %reshape.418 = f32[256,1,2,32,64]{4,3,2,1,0:T(8,128)} reshape(f32[2,524288]{1,0:T(2,128)} %reduce.8) | data formatting | bytes 8388608
  364.9 7.7 copy.61
  372.6 9.6 %convolution_bitcast_fusion.1 = f32[1,2,32,128,256]{3,4,2,1,0:T(8,128)S(1)} fusion(f32[2,128,32,128,1]{3,1,0,2,4:T(8,128)} %bitcast.224, f32[1,256,2,128]{3,1,2,0:T(8,128)S(1)} %get-tuple-element.21, f32[1,256,2,128]{3,1,2,0:T(8,128)S(1)} %get-tuple-element.20), kind=kOutput, calls=%fused_computation.9 | convolution fusion | flops 6442582016 | bytes 13107200 | tf_op jit(solution)/shard_map/fclxy,dkcl->fdxyk/dot_general | solution.py:25
  382.2 8.1 copy.62
  396.4 16.6 %reduce.5 = f32[2,524288]{1,0:T(2,128)} reduce(f32[2,1,524288]{2,1,0:T(1,128)} %all-to-all-done.2, f32[]{:T(128)} %broadcast.301), dimensions={1}, to_apply=%all_to_all.94.reduce_sub_computation | reduce | bytes 8388612 | tf_op jit(solution)/shard_map/all_to_all | solution.py:41
  413.0 10.1 %reshape.412 = f32[256,1,2,32,64]{4,3,2,1,0:T(8,128)} reshape(f32[2,524288]{1,0:T(2,128)} %reduce.5) | data formatting | bytes 8388608
  423.1 7.7 copy.49
  430.8 9.5 %convolution_bitcast_fusion.2 = f32[1,2,32,128,256]{3,4,2,1,0:T(8,128)S(1)} fusion(f32[2,128,32,128,1]{3,1,0,2,4:T(8,128)} %bitcast.225, f32[1,256,2,128]{3,1,2,0:T(8,128)S(1)} %get-tuple-element.21, f32[1,256,2,128]{3,1,2,0:T(8,128)S(1)} %get-tuple-element.20), kind=kOutput, calls=%fused_computation.10 | convolution fusion | flops 6442582016 | bytes 13107200 | tf_op jit(solution)/shard_map/fclxy,dkcl->fdxyk/dot_general | solution.py:25
  440.3 8.3 copy.50
  448.6 130.5 %all-to-all-done.7 = f32[1,2,32,128,256]{3,2,1,0,4:T(8,128)} async-done(((f32[1,2,32,128,256]{3,2,1,0,4:T(8,128)}), f32[1,2,32,128,256]{3,2,1,0,4:T(8,128)}, u32[]{:S(2)}, u32[]{:S(2)}) %all-to-all-start.7) | async-done | bytes 8388640 | tf_op jit(solution)/shard_map/all_to_all | solution.py:33
  589.4 17.1 %convolution_bitcast_fusion = f32[1,2,128,64,256]{2,4,3,1,0:T(8,128)} fusion(f32[2,128,128,64,1]{2,1,0,3,4:T(8,128)S(1)} %bitcast.219, f32[1,256,2,128]{3,1,2,0:T(8,128)S(1)} %get-tuple-element.21, f32[1,256,2,128]{3,1,2,0:T(8,128)S(1)} %get-tuple-element.20), kind=kOutput, calls=%fused_computation.3 | convolution fusion | flops 12885032960 | bytes 25690112 | tf_op jit(solution)/shard_map/fclxy,dkcl->fdxyk/dot_general | solution.py:25
  606.5 161.1 %all-to-all-done.3 = f32[1,2,32,128,256]{3,2,1,0,4:T(8,128)} async-done(((f32[1,2,32,128,256]{3,2,1,0,4:T(8,128)}), f32[1,2,32,128,256]{3,2,1,0,4:T(8,128)}, u32[]{:S(2)}, u32[]{:S(2)}) %all-to-all-start.3) | async-done | bytes 8388640 | tf_op jit(solution)/shard_map/all_to_all | solution.py:33
  772.0 17.0 %fusion.32 = f32[2,256,128,64,1]{2,1,4,3,0:T(8,128)} fusion(f32[2,128,128,64,1]{2,1,0,3,4:T(8,128)S(1)} %bitcast.218, f32[1,256,2,128]{3,1,2,0:T(8,128)S(1)} %get-tuple-element.21, f32[1,256,2,128]{3,1,2,0:T(8,128)S(1)} %get-tuple-element.20), kind=kOutput, calls=%fused_computation.66 | convolution fusion | flops 12885032960 | bytes 25690112 | tf_op jit(solution)/shard_map/fclxy,dkcl->fdxyk/dot_general | solution.py:25
  789.0 19.3 %subtract_bitcast_fusion = (f32[1,128,64,256]{1,3,2,0:T(8,128)}, f32[1,128,64,256]{1,3,2,0:T(8,128)}) fusion(f32[1,2,128,64,256]{2,4,3,1,0:T(8,128)} %convolution_bitcast_fusion, f32[1,2,128,64,256]{2,4,3,1,0:T(8,128)} %bitcast.216), kind=kLoop, calls=%fused_computation.2 | loop fusion | flops 12582912 | bytes 50331648 | tf_op jit(solution)/shard_map/sub | solution.py:53
  808.3 11.8 %maximum_bitcast_fusion = f32[1,2,128,64,256]{2,4,3,1,0:T(8,128)} fusion(f32[1,128,64,256]{1,3,2,0:T(8,128)} %get-tuple-element.15, f32[1,128,64,256]{1,3,2,0:T(8,128)} %get-tuple-element.14), kind=kLoop, calls=%fused_computation | loop fusion | flops 4194304 | bytes 33554432 | tf_op jit(solution)/shard_map/broadcast_in_dim | solution.py:80
  820.1 17.4 %copy.65 = f32[1,2,128,64,256]{4,3,2,1,0:T(8,128)} copy(f32[1,2,128,64,256]{2,4,3,1,0:T(8,128)} %maximum_bitcast_fusion) | data formatting | bytes 33554432
  837.4 17.4 %copy.64 = f32[2,128,64,256]{3,2,1,0:T(8,128)} copy(f32[2,128,64,256]{1,3,2,0:T(8,128)} %bitcast.217) | data formatting | bytes 33554432
  (60 shorter events, 174.5 us)
Async XLA Ops:
  7.2 1.6 slice-start
  24.4 103.1 %all-to-all-start.4 = ((f32[4,1,131072]{2,1,0:T(1,128)}), f32[4,1,131072]{2,1,0:T(1,128)}, u32[]{:S(2)}, u32[]{:S(2)}) async-start(f32[4,1,131072]{2,1,0:T(1,128)} %reshape.413), calls=%async_computation.4 | async-start | bytes 4194304 | tf_op jit(solution)/shard_map/all_to_all | solution.py:33
  30.8 82.7 %all-reduce.3.cloned.1.call-start = ((), (), s32[]{:S(2)}) async-start(), calls=%async_computation.8 | async-start | bytes 6291456 | tf_op jit(solution)/shard_map/psum | solution.py:73
  127.5 52.9 %all-to-all-start = ((f32[4,1,131072]{2,1,0:T(1,128)}), f32[4,1,131072]{2,1,0:T(1,128)}, u32[]{:S(2)}, u32[]{:S(2)}) async-start(f32[4,1,131072]{2,1,0:T(1,128)} %reshape.407), calls=%async_computation | async-start | bytes 4194304 | tf_op jit(solution)/shard_map/all_to_all | solution.py:33
  180.4 41.6 %all-to-all-start.5 = ((f32[2,1,262144]{2,1,0:T(1,128)}), f32[2,1,262144]{2,1,0:T(1,128)}, u32[]{:S(2)}, u32[]{:S(2)}) async-start(f32[2,1,262144]{2,1,0:T(1,128)} %reshape.415), calls=%async_computation.5 | async-start | bytes 4194304 | tf_op jit(solution)/shard_map/all_to_all | solution.py:41
  222.0 55.5 %all-to-all-start.1 = ((f32[2,1,262144]{2,1,0:T(1,128)}), f32[2,1,262144]{2,1,0:T(1,128)}, u32[]{:S(2)}, u32[]{:S(2)}) async-start(f32[2,1,262144]{2,1,0:T(1,128)} %reshape.409), calls=%async_computation.1 | async-start | bytes 4194304 | tf_op jit(solution)/shard_map/all_to_all | solution.py:41
  251.9 1.9 copy-start
  277.6 54.8 %all-to-all-start.6 = ((f32[2,1,524288]{2,1,0:T(1,128)}), f32[2,1,524288]{2,1,0:T(1,128)}, u32[]{:S(2)}, u32[]{:S(2)}) async-start(f32[2,1,524288]{2,1,0:T(1,128)} %reshape.417), calls=%async_computation.6 | async-start | bytes 8388608 | tf_op jit(solution)/shard_map/all_to_all | solution.py:41
  332.4 57.9 %all-to-all-start.2 = ((f32[2,1,524288]{2,1,0:T(1,128)}), f32[2,1,524288]{2,1,0:T(1,128)}, u32[]{:S(2)}, u32[]{:S(2)}) async-start(f32[2,1,524288]{2,1,0:T(1,128)} %reshape.411), calls=%async_computation.2 | async-start | bytes 8388608 | tf_op jit(solution)/shard_map/all_to_all | solution.py:41
  390.3 188.8 %all-to-all-start.7 = ((f32[1,2,32,128,256]{3,2,1,0,4:T(8,128)}), f32[1,2,32,128,256]{3,2,1,0,4:T(8,128)}, u32[]{:S(2)}, u32[]{:S(2)}) async-start(f32[1,2,32,128,256]{3,2,1,0,4:T(8,128)} %copy.62), calls=%async_computation.7 | async-start | bytes 16777216 | tf_op jit(solution)/shard_map/all_to_all | solution.py:33
  579.0 188.5 %all-to-all-start.3 = ((f32[1,2,32,128,256]{3,2,1,0,4:T(8,128)}), f32[1,2,32,128,256]{3,2,1,0,4:T(8,128)}, u32[]{:S(2)}, u32[]{:S(2)}) async-start(f32[1,2,32,128,256]{3,2,1,0,4:T(8,128)} %copy.50), calls=%async_computation.3 | async-start | bytes 16777216 | tf_op jit(solution)/shard_map/all_to_all | solution.py:33
Sparse Core Ops, SparseCore 0:
  43.5 69.9 all-reduce.2
where the time goes:
time: 869 us; the launch traced here: 862 us
  waiting for transfers between devices  373 us (43%)
  local copies, waits for them, and re-layouts  242 us (28%)
  other arithmetic  107 us (12%)
  matrix products  80.8 us (9%)
  starting transfers between devices  44.5 us (5%)
  between operations  14.5 us (2%)
    all_to_all x4, waiting for transfers between devices, turn_depth(): lax.all_to_all(values, 'pz', split_axis=4, concat_axis=2, tiled=True)  302 us
    unnamed x16, local copies, waits for them, and re-layouts  110 us
    psum x1, waiting for transfers between devices, on_device(): lax.psum((numer_real, numer_imag, denominator), 'tx')  70.1 us
    dot_general x8, matrix products, remote_step(): jnp.einsum('fclxy,dkcl->fdxyk', values, matrix, precision=lax.Precision.H...  63.5 us
    all_to_all x4, other arithmetic, turn_height(): lax.all_to_all(values, 'py', split_axis=4, concat_axis=2, tiled=True)  49.7 us
    all_to_all x4, local copies, waits for them, and re-layouts, turn_height(): lax.all_to_all(values, 'py', split_axis=4, concat_axis=2, tiled=True)  30.2 us
    transpose x4, local copies, waits for them, and re-layouts, local_step(): jnp.einsum('fcxyl,dkcl->fdyxk', values, matrix, precision=lax.Precision.H...  28.2 us
    transpose x4, local copies, waits for them, and re-layouts, remote_step(): jnp.einsum('fclxy,dkcl->fdxyk', values, matrix, precision=lax.Precision.H...  27.4 us
  transfers between devices with their start and end apart: 9, of which 4 were waited for; matrix products, arithmetic and copies ran while one was open for 38% of the time, Pallas kernels for 0%

commit v1 on v0

v1 whole, which is shorter than its diff:
```python
import functools
import math

import jax
import jax.numpy as jnp
import ml_dtypes
import numpy as np
from jax import lax
from jax.experimental import pallas as pl
from jax.experimental.pallas import tpu as pltpu
from jax.sharding import PartitionSpec as P

F32 = jnp.float32
BF16 = jnp.bfloat16
NN = (((1,), (0,)), ((), ()))
NT = (((1,), (1,)), ((), ()))


def signed(count):
    index = np.arange(count)
    return np.where(index < count // 2, index, index - count)


def forward_matrix(coarse):
    index = np.arange(coarse)
    return np.exp(-2j * np.pi * ((index[:, None] * index[None, :]) % coarse) / coarse)


def inverse_matrix(coarse, fine):
    phases = (np.arange(fine)[:, None] * signed(coarse)[None, :]) % fine
    return np.exp(2j * np.pi * phases / fine) / coarse


def halves(matrix):
    high = matrix.astype(ml_dtypes.bfloat16)
    low = (matrix - high.astype(np.float64)).astype(ml_dtypes.bfloat16)
    return np.stack([high, low], axis=-3)


def block_form(matrix):
    re, im = matrix.real, matrix.imag
    return np.stack([np.stack([re, -im], 1), np.stack([im, re], 1)], 0)


def split(x):
    high = x.astype(BF16)
    return high, (x - high.astype(F32)).astype(BF16)


def product_left(m_ref, x, dims):
    high, low = split(x)
    mh, ml = m_ref[0], m_ref[1]
    dot = functools.partial(lax.dot_general, dimension_numbers=dims, preferred_element_type=F32)
    return dot(mh, high) + dot(mh, low) + dot(ml, high)


def product_right(x, m_ref):
    high, low = split(x)
    mh, ml = m_ref[0], m_ref[1]
    dot = functools.partial(lax.dot_general, dimension_numbers=NN, preferred_element_type=F32)
    return dot(high, mh) + dot(low, mh) + dot(high, ml)


def times_i(x):
    half = x.shape[1] // 2
    return jnp.concatenate([-x[:, half:], x[:, :half]], axis=1)


def depth_forward(m_ref, x_ref, o_ref):
    parts, _, rows, _ = o_ref.shape
    for s in range(x_ref.shape[3]):
        re, im = x_ref[0, 0, :, s, :], x_ref[0, 1, :, s, :]
        both = jnp.concatenate(
            [jnp.concatenate([re, -im], axis=1), jnp.concatenate([im, re], axis=1)], axis=0
        )
        out = product_left(m_ref, both, NT)
        for p in range(parts):
            o_ref[p, s] = out[p * rows : (p + 1) * rows]


def middle_forward(m_ref, x_ref, o_ref):
    parts, _, rows, lanes = o_ref.shape
    for s in range(x_ref.shape[2]):
        x = x_ref[:, :, s, :].reshape(-1, lanes)
        out = product_left(m_ref, jnp.concatenate([x, times_i(x)], axis=0), NN)
        for p in range(parts):
            o_ref[p, s] = out[p * rows : (p + 1) * rows]


def top_forward(m_ref, x_ref, g_ref, o_ref):
    parts, count, rows, lanes = x_ref.shape
    x = jnp.concatenate([x_ref[p].reshape(count * rows, lanes) for p in range(parts)], axis=1)
    v = product_right(x, m_ref)
    coarse = v.shape[1] // 2
    vr, vi = v[:, :coarse], v[:, coarse:]
    gr, gi = g_ref[0].reshape(count * rows, coarse), g_ref[1].reshape(count * rows, coarse)
    wr = vr * gr - vi * gi
    wi = vr * gi + vi * gr
    wide = coarse // parts
    for p in range(parts):
        cut = slice(p * wide, (p + 1) * wide)
        o_ref[p] = jnp.concatenate([wr[:, cut], wi[:, cut]], axis=1).reshape(count, rows, lanes)


def middle_inverse(m_ref, x_ref, *o_refs):
    parts, _, rows, lanes = o_refs[0].shape
    for s in range(x_ref.shape[1]):
        x = jnp.concatenate([x_ref[p, s] for p in range(x_ref.shape[0])], axis=0)
        out = product_left(m_ref, jnp.concatenate([x, times_i(x)], axis=0), NN)
        for p in range(parts):
            for h, o_ref in enumerate(o_refs):
                at = (p * len(o_refs) + h) * rows
                o_ref[p, s] = out[at : at + rows]


def middle_refine(m_ref, x_ref, o_ref):
    rows = o_ref.shape[2]
    for i in range(x_ref.shape[2]):
        pieces = [x_ref[q, c, i] for q in range(x_ref.shape[0]) for c in range(2)]
        out = product_left(m_ref, jnp.concatenate(pieces, axis=0), NN)
        o_ref[0, i] = out[:rows]
        o_ref[1, i] = out[rows:]


def last_product(t, m_ref):
    top = t.shape[0] // 2
    out = product_right(jnp.concatenate([t[:top], t[top:]], axis=1), m_ref)
    fine = out.shape[1] // 2
    return out[:, :fine], out[:, fine:]


def contrast_last(m1_ref, m3_ref, *refs):
    *x_refs, o_ref = refs
    lanes = x_refs[0].shape[3]
    for s in range(o_ref.shape[2]):
        x = jnp.concatenate([r[:, :, s, :].reshape(-1, lanes) for r in x_refs], axis=0)
        re, im = last_product(product_left(m1_ref, x, NN), m3_ref)
        o_ref[0, :, s, :] = re
        o_ref[1, :, s, :] = im


def scatter_last(slots, m1_ref, m3_ref, c_ref, *refs):
    x_refs, o_ref = refs[:slots], refs[-1]
    lanes = x_refs[0].shape[3]
    for s in range(o_ref.shape[3]):
        x = jnp.concatenate([r[:, :, s, :].reshape(-1, lanes) for r in x_refs], axis=1)
        re, im = last_product(product_left(m1_ref, x, NT), m3_ref)
        cr, ci = c_ref[0, :, s, :], c_ref[1, :, s, :]
        o_ref[0, 0, :, s, :] = cr * re - ci * im
        o_ref[0, 1, :, s, :] = cr * im + ci * re


def whole(array):
    zeros = (0,) * array.ndim
    return pl.BlockSpec(array.shape, lambda i: zeros)


def along(shape, axis, block, offset=0):
    sizes = tuple(block if a == axis else n for a, n in enumerate(shape))
    return pl.BlockSpec(sizes, lambda i: tuple(i + offset if a == axis else 0 for a in range(len(shape))))


def call(body, steps, in_specs, operands, shapes, out_specs, name, flops, aliases=None):
    moved = sum(math.prod(s.shape) * 4 for s in shapes) * 2
    return pl.pallas_call(
        body,
        grid=(steps,),
        in_specs=in_specs,
        out_specs=out_specs,
        out_shape=shapes,
        input_output_aliases=aliases or {},
        name=name,
        cost_estimate=pl.CostEstimate(flops=flops, bytes_accessed=moved, transcendentals=0),
        compiler_params=pltpu.CompilerParams(vmem_limit_bytes=56 * 2**20),
    )(*operands)


ROWS = 8


def shape_of(*dims):
    return jax.ShapeDtypeStruct(dims, F32)


def exchange(x, axis):
    return lax.all_to_all(x, axis, 0, 0, tiled=True)


def swap(x, axis, size, bit):
    return lax.ppermute(x, axis, [(i, i ^ bit) for i in range(size)])


def gather_slots(pieces, axis, size):
    bit = size // 2
    order = [(0, p) for p in pieces]
    while bit:
        order = order + [(j | bit, swap(p, axis, size, bit)) for j, p in order]
        bit //= 2
    return order


def aligned_device(tx, py, pz, chunks, fields, sources, green):
    coarse = fields.shape[4]
    fine = 2 * coarse
    x1, x2 = fields.shape[2], fields.shape[3]
    f1, f2 = fine // py, fine // pz
    lanes = 2 * x1
    part = x1 // tx
    k3 = coarse // pz
    me_y, me_z, me_x = lax.axis_index("py"), lax.axis_index("pz"), lax.axis_index("tx")

    fwd, inv = forward_matrix(coarse), inverse_matrix(coarse, fine)
    refine = inv @ fwd
    ri = lambda m: np.concatenate([m.real, m.imag], axis=1)
    m_fwd = jnp.asarray(halves(ri(fwd)))
    m_inv = jnp.asarray(halves(ri(inv)))
    top = block_form(fwd).reshape(2 * coarse, 2, py, x1).transpose(2, 1, 3, 0)
    m_top = jnp.asarray(halves(top.reshape(2 * coarse, 2 * coarse)))
    last = block_form(inv).transpose(2, 3, 0, 1).reshape(2 * coarse, 2 * fine)
    m_last = jnp.asarray(halves(last))
    last_c = block_form(refine).transpose(2, 3, 0, 1).reshape(2 * coarse, 2 * fine)
    m_last_c = jnp.asarray(halves(last_c))
    first = block_form(inv).reshape(2, py, f1, 2, py, x1)
    m_first = jnp.asarray(
        halves(
            np.stack(
                [
                    first[:, y][:, :, :, [y ^ j for j in range(py)]].transpose(0, 1, 3, 2, 4)
                    .reshape(2 * f1, 2 * coarse)
                    for y in range(py)
                ]
            )
        )
    )[me_y]
    mid = block_form(refine).reshape(2, pz, f2, 2, pz, x2).transpose(1, 0, 2, 4, 3, 5)
    m_mid = jnp.asarray(halves(mid.reshape(pz, 2 * f2, 2 * coarse)))[me_z]

    fr, fi, sr, si = fields[:, 0], fields[:, 1], sources[:, 0], sources[:, 1]
    numer_re = jnp.sum(sr * fr + si * fi, axis=0)
    numer_im = jnp.sum(si * fr - sr * fi, axis=0)
    denom = jnp.sum(fr * fr + fi * fi, axis=0)
    cut = lambda v: v.reshape(tx, part, x2, coarse)
    sums = exchange(jnp.stack([cut(numer_re), cut(numer_im), cut(denom)], axis=1), "tx")
    sums = jnp.sum(sums, axis=0)
    contrast = sums[:2] / sums[2:]

    spec = call(
        depth_forward, x2 // ROWS,
        [whole(m_fwd), pl.BlockSpec((1, 2, x1, ROWS, coarse), lambda i: (0, 0, 0, i, 0))],
        (m_fwd, sources), [shape_of(pz, x2, k3, lanes)], [along((pz, x2, k3, lanes), 1, ROWS)],
        "depth_forward", 6 * 2 * x2 * coarse * coarse * lanes,
    )[0]
    spec = exchange(spec, "pz")
    spec = call(
        middle_forward, k3 // ROWS,
        [whole(m_fwd), along(spec.shape, 2, ROWS)],
        (m_fwd, spec), [shape_of(py, k3, x1, lanes)], [along((py, k3, x1, lanes), 1, ROWS)],
        "middle_forward", 6 * 2 * k3 * coarse * coarse * lanes,
    )[0]
    spec = exchange(spec, "py")
    spec = call(
        top_forward, k3 // ROWS,
        [whole(m_top), along(spec.shape, 1, ROWS), along(green.shape, 1, ROWS)],
        (m_top, spec, green), [shape_of(py, k3, x1, lanes)], [along((py, k3, x1, lanes), 1, ROWS)],
        "top_forward", 6 * 4 * k3 * x1 * coarse * coarse,
    )[0]
    spec = exchange(spec, "py")

    some = f2 // chunks
    dims = (pz, k3, some, lanes)
    pieces = call(
        middle_inverse, k3 // ROWS,
        [whole(m_inv), along(spec.shape, 1, ROWS)],
        (m_inv, spec), [shape_of(*dims)] * chunks, [along(dims, 1, ROWS)] * chunks,
        "middle_inverse", 6 * 2 * k3 * fine * coarse * lanes,
    )

    spread = jnp.broadcast_to(contrast[None], (pz,) + contrast.shape)
    seen = exchange(spread, "pz")
    ref_dims = (2, part, f2, coarse)
    step = min(4, part)
    mine = call(
        middle_refine, part // step,
        [whole(m_mid), along(seen.shape, 2, step)],
        (m_mid, seen), [shape_of(*ref_dims)], [along(ref_dims, 1, step)],
        "middle_refine", 6 * 4 * part * f2 * coarse * coarse,
    )[0]
    slots = []
    for j, piece in gather_slots([mine], "py", py):
        slots += [(j, piece)]
    order, parts = [s[0] for s in slots], [s[1] for s in slots]
    bit, codes = tx // 2, [(j, 0) for j in order]
    while bit:
        parts = parts + [swap(p, "tx", tx, bit) for p in parts]
        codes = codes + [(j, t | bit) for j, t in codes]
        bit //= 2
    dim1 = block_form(refine).reshape(2, py, f1, 2, py, tx, part)
    table = np.stack(
        [
            np.stack(
                [dim1[:, y][:, :, :, y ^ j, t ^ k] for j, k in codes], axis=2
            ).reshape(2 * f1, 2 * coarse)
            for y in range(py)
            for t in range(tx)
        ]
    )
    m_first_c = jnp.asarray(halves(table))[me_y * tx + me_x]
    out_dims = (2, f1, f2, fine)
    contrast_fine = call(
        contrast_last, f2 // ROWS,
        [whole(m_first_c), whole(m_last_c)] + [along(ref_dims, 2, ROWS)] * len(parts),
        (m_first_c, m_last_c, *parts), [shape_of(*out_dims)], [along(out_dims, 2, ROWS)],
        "contrast_last", 6 * 8 * f1 * f2 * coarse * fine,
    )[0]

    scattered = None
    scat_dims = (1,) + out_dims
    for h, piece in enumerate(pieces):
        piece = exchange(piece, "pz")
        arrived = [p for _, p in gather_slots([piece], "py", py)]
        offset = h * some // ROWS
        specs = [whole(m_first), whole(m_last), along(out_dims, 2, ROWS, offset)]
        specs += [along(dims, 2, ROWS)] * py
        operands = (m_first, m_last, contrast_fine, *arrived)
        aliases = None
        if scattered is not None:
            aliases = {len(operands): 0}
            specs += [pl.BlockSpec(memory_space=pl.ANY)]
            operands += (scattered,)
        scattered = call(
            functools.partial(scatter_last, py), some // ROWS, specs, operands,
            [shape_of(*scat_dims)], [along(scat_dims, 3, ROWS, offset)],
            "scatter_last", 6 * 8 * f1 * some * coarse * fine, aliases,
        )[0]
    return contrast_fine, scattered


def fourier_matrix(out_index, in_index, period, exponent_sign, weight):
    phases = out_index[:, None] * in_index[None, :] % period
    angles = exponent_sign * 2.0 * math.pi / period * phases.astype(jnp.float32)
    cosine = weight * jnp.cos(angles)
    sine_part = weight * jnp.sin(angles)
    return jnp.stack([jnp.stack([cosine, -sine_part], 1), jnp.stack([sine_part, cosine], 1)], 0)


def local_step(values, matrix):
    return jnp.einsum("fcxyl,dkcl->fdyxk", values, matrix, precision=lax.Precision.HIGHEST)


def remote_step(values, matrix):
    return jnp.einsum("fclxy,dkcl->fdxyk", values, matrix, precision=lax.Precision.HIGHEST)


def turn(values, matrix, axis):
    return remote_step(lax.all_to_all(values, axis, split_axis=4, concat_axis=2, tiled=True), matrix)


def forward_pass(values, matrix):
    return turn(turn(local_step(values, matrix), matrix, "pz"), matrix, "py")


def inverse_pass(values, matrix):
    return turn(turn(local_step(values, matrix), matrix, "py"), matrix, "pz")


def complex_product(first_factor, second_factor):
    real_part = first_factor[0] * second_factor[0] - first_factor[1] * second_factor[1]
    imag_part = first_factor[0] * second_factor[1] + first_factor[1] * second_factor[0]
    return jnp.stack([real_part, imag_part])


def general_device(fields, sources, green):
    coarse = fields.shape[4]
    fine = 2 * coarse
    index = jnp.arange(coarse, dtype=jnp.int32)
    fine_index = jnp.arange(fine, dtype=jnp.int32)
    signed_coarse = jnp.where(index < coarse // 2, index, index - coarse)
    unit_coarse = jnp.ones((coarse, 1), F32)
    unit_fine = jnp.ones((fine, 1), F32)
    coarse_forward = fourier_matrix(index, index, coarse, -1.0, unit_coarse)
    padded_inverse = fourier_matrix(fine_index, signed_coarse, fine, 1.0, unit_fine / coarse)
    fr, fi, sr, si = fields[:, 0], fields[:, 1], sources[:, 0], sources[:, 1]
    numer_re = jnp.sum(sr * fr + si * fi, axis=0)
    numer_im = jnp.sum(si * fr - sr * fi, axis=0)
    denom = jnp.sum(fr * fr + fi * fi, axis=0)
    numer_re, numer_im, denom = lax.psum((numer_re, numer_im, denom), "tx")
    contrast = jnp.stack([numer_re / denom, numer_im / denom])[None]
    contrast_fine = inverse_pass(forward_pass(contrast, coarse_forward), padded_inverse)[0]
    spectrum = forward_pass(sources[0:1], coarse_forward)
    weighted = complex_product(spectrum[0], green)[None]
    domain_field = inverse_pass(weighted, padded_inverse)[0]
    return contrast_fine, complex_product(contrast_fine, domain_field)[None]


def power_of_two(n):
    return n & (n - 1) == 0


def solution(mesh):
    tx, py, pz = mesh.shape["tx"], mesh.shape["py"], mesh.shape["pz"]
    chunks = 2

    def on_device(fields, sources, green):
        x1, x2, coarse = fields.shape[2:]
        fine_block = 2 * coarse // pz
        aligned = (
            power_of_two(tx) and power_of_two(py) and coarse % 128 == 0
            and (2 * x1) % 128 == 0 and x1 % tx == 0 and x2 % ROWS == 0
            and fine_block % (chunks * ROWS) == 0
        )
        if aligned:
            return aligned_device(tx, py, pz, chunks, fields, sources, green)
        return general_device(fields, sources, green)

    placed = (
        P("tx", None, "py", "pz", None),
        P("tx", None, "py", "pz", None),
        P(None, "pz", "py", None),
    )
    return jax.shard_map(
        on_device,
        mesh=mesh,
        in_specs=placed,
        out_specs=(P(None, "py", "pz", None), P("tx", None, "py", "pz", None)),
        check_vma=False,
    )
```

time: 869 us -> 440 us (0.51)
  local copies, waits for them, and re-layouts: 242 us -> 9.15 us
  waiting for transfers between devices: 373 us -> 200 us
  blocking collectives: 0 us -> 106 us
  other arithmetic: 107 us -> 11.7 us
  Pallas kernels: 0 us -> 84.9 us
  matrix products: 80.8 us -> 0 us
  starting transfers between devices: 44.5 us -> 26 us
  between operations: 14.5 us -> 0.72 us
    all_to_all x8 -> x5, waiting for transfers between devices: 302 us -> 109 us  [exchange(): return lax.all_to_all(x, axis, 0, 0, tiled=True)]
    unnamed x16 -> x8, local copies, waits for them, and re-layouts: 110 us -> 2.64 us
    all_to_all x0 -> x2, blocking collectives: none -> 106 us  [exchange(): return lax.all_to_all(x, axis, 0, 0, tiled=True)]
    ppermute x0 -> x9, waiting for transfers between devices: none -> 91.9 us  [swap(): return lax.ppermute(x, axis, [(i, i ^ bit) for i in range(size)])]
    pallas_call x0 -> x8, Pallas kernels: none -> 84.9 us  [call(): pl.pallas_call(body, grid=(steps,), in_specs=in_specs, out_specs=out_spec...]
    dot_general x12 -> x0, matrix products: 80.8 us -> none  [the longest x8 63.5 us: remote_step(): jnp.einsum('fclxy,dkcl->fdxyk', values, matrix, precision=lax.Precision.H...]
    psum x1 -> x0, waiting for transfers between devices: 70.1 us -> none  [on_device(): lax.psum((numer_real, numer_imag, denominator), 'tx')]
    all_to_all x6 -> x0, other arithmetic: 65.2 us -> none  [the longest x4 49.7 us: turn_height(): lax.all_to_all(values, 'py', split_axis=4, concat_axis=2, tiled=True)]
  transfers between devices with their start and end apart: 9 -> 14, of which waited for: 4 -> 8; matrix products, arithmetic and copies ran while one was open for 38% -> 4% of each run, Pallas kernels for 0% -> 13%
where the time goes in v1:
time: 440 us; the launch traced here: 439 us
  waiting for transfers between devices  200 us (45%)
  blocking collectives  106 us (24%)
  Pallas kernels  84.9 us (19%)
  starting transfers between devices  26 us (6%)
  other arithmetic  11.7 us (3%)
  local copies, waits for them, and re-layouts  9.15 us (2%)
    all_to_all x5, waiting for transfers between devices, exchange(): return lax.all_to_all(x, axis, 0, 0, tiled=True)  109 us
    all_to_all x2, blocking collectives, exchange(): return lax.all_to_all(x, axis, 0, 0, tiled=True)  106 us
    ppermute x9, waiting for transfers between devices, swap(): return lax.ppermute(x, axis, [(i, i ^ bit) for i in range(size)])  91.9 us
    pallas_call x8, Pallas kernels, call(): pl.pallas_call(body, grid=(steps,), in_specs=in_specs, out_specs=out_spec...  84.9 us
    all_to_all x5, starting transfers between devices, exchange(): return lax.all_to_all(x, axis, 0, 0, tiled=True)  20.6 us
  transfers between devices with their start and end apart: 14, of which 8 were waited for; matrix products, arithmetic and copies ran while one was open for 4% of the time, Pallas kernels for 13%

profile of v1, /device:TPU:0, one launch (start us, length us, event | category | flops | bytes accessed | tf_op | source)
XLA Modules:
  0.0 438.9 jit_solution(15308392783602494121)
XLA Ops:
  0.6 5.8 %depth_forward.1 = f32[4,32,32,128]{3,2,1,0:T(8,128)} custom-call(bf16[2,128,256]{2,1,0:T(8,128)(2,1)} %constant.38.clone.m_ref, f32[4,2,64,32,128]{4,3,2,1,0:T(8,128)} %x_ref.1), custom_call_target="tpu_custom_call" | custom-call | flops 805306368 | bytes 4194304 | tf_op jit(solution)/shard_map/depth_forward/pallas_call | solution.py:165
  6.4 54.6 %all_to_all.35.x_ref = f32[4,32,32,128]{3,2,1,0:T(8,128)} all-to-all(f32[4,32,32,128]{3,2,1,0:T(8,128)} %depth_forward.1), channel_id=1, replica_groups=mesh['tx'=4,'py'=2,'pz'=4] {'pz'}, dimensions={0} | all-to-all | bytes 4194304 | tf_op jit(solution)/shard_map/all_to_all | solution.py:186
  61.1 6.4 %middle_forward.1 = f32[2,32,64,128]{3,2,1,0:T(8,128)} custom-call(bf16[2,128,256]{2,1,0:T(8,128)(2,1)} %constant.38.clone.m_ref, f32[4,32,32,128]{3,2,1,0:T(8,128)} %all_to_all.35.x_ref), custom_call_target="tpu_custom_call" | custom-call | flops 805306368 | bytes 4194304 | tf_op jit(solution)/shard_map/middle_forward/pallas_call | solution.py:165
  67.5 3.8 all-to-all-start.3
  71.2 7.3 %add_reduce_fusion.1 = (f32[64,32,128]{2,1,0:T(8,128)S(1)}, f32[64,32,128]{2,1,0:T(8,128)S(1)}, f32[64,32,128]{2,1,0:T(8,128)S(1)}) fusion(f32[4,2,64,32,128]{4,3,2,1,0:T(8,128)} %x_ref.1, f32[4,2,64,32,128]{4,3,2,1,0:T(8,128)} %param.11), kind=kLoop, calls=%fused_computation.2 | loop fusion | flops 11796480 | bytes 19922944 | tf_op jit(solution)/shard_map/reduce_sum | solution.py:239
  78.6 2.0 pad_maximum_fusion
  80.5 14.7 %all-to-all-done.3.x_ref = f32[2,32,64,128]{3,2,1,0:T(8,128)S(1)} async-done(((f32[2,32,64,128]{3,2,1,0:T(8,128)}), f32[2,32,64,128]{3,2,1,0:T(8,128)S(1)}, u32[]{:S(2)}, u32[]{:S(2)}) %all-to-all-start.3) | async-done | bytes 2097184 | tf_op jit(solution)/shard_map/all_to_all | solution.py:186
  95.3 1.3 copy-done.1
  96.6 3.7 all-to-all-start
  100.3 5.1 %top_forward.1 = f32[2,32,64,128]{3,2,1,0:T(8,128)} custom-call(bf16[2,256,256]{2,1,0:T(8,128)(2,1)} %constant.40.clone.m_ref, f32[2,32,64,128]{3,2,1,0:T(8,128)} %copy-done.1, f32[2,32,64,128]{3,2,1,0:T(8,128)} %g_ref.1), custom_call_target="tpu_custom_call" | custom-call | flops 805306368 | bytes 4194304 | tf_op jit(solution)/shard_map/top_forward/pallas_call | solution.py:165
  105.4 31.8 %all-to-all-done = f32[4,3,16,32,128]{4,3,2,1,0:T(8,128)S(1)} async-done(((f32[4,3,16,32,128]{4,3,2,1,0:T(8,128)}), f32[4,3,16,32,128]{4,3,2,1,0:T(8,128)S(1)}, u32[]{:S(2)}, u32[]{:S(2)}) %all-to-all-start) | async-done | bytes 3145760 | tf_op jit(solution)/shard_map/all_to_all | solution.py:186
  137.2 4.8 %all-to-all-start.4 = ((f32[2,32,64,128]{3,2,1,0:T(8,128)}), f32[2,32,64,128]{3,2,1,0:T(8,128)}, u32[]{:S(2)}, u32[]{:S(2)}) async-start(f32[2,32,64,128]{3,2,1,0:T(8,128)} %top_forward.1), calls=%async_computation.4 | async-start | bytes 4194304 | tf_op jit(solution)/shard_map/all_to_all | solution.py:186
  142.0 1.3 reduce_sum.39
  145.3 21.5 %all-to-all-done.4.x_ref = f32[2,32,64,128]{3,2,1,0:T(8,128)} async-done(((f32[2,32,64,128]{3,2,1,0:T(8,128)}), f32[2,32,64,128]{3,2,1,0:T(8,128)}, u32[]{:S(2)}, u32[]{:S(2)}) %all-to-all-start.4) | async-done | bytes 2097184 | tf_op jit(solution)/shard_map/all_to_all | solution.py:186
  166.9 1.6 broadcast_in_dim.2
  168.5 3.6 all-to-all-start.1
  172.1 6.8 %middle_inverse.1 = (f32[4,32,32,128]{3,2,1,0:T(8,128)}, f32[4,32,32,128]{3,2,1,0:T(8,128)}) custom-call(bf16[2,256,256]{2,1,0:T(8,128)(2,1)} %constant.39.clone.m_ref, f32[2,32,64,128]{3,2,1,0:T(8,128)} %all-to-all-done.4.x_ref), custom_call_target="tpu_custom_call" | custom-call | flops 1610612736 | bytes 8388608 | tf_op jit(solution)/shard_map/middle_inverse/pallas_call | solution.py:165
  178.9 40.5 %all-to-all-done.1.x_ref = f32[4,2,16,32,128]{4,3,2,1,0:T(8,128)S(1)} async-done(((f32[4,2,16,32,128]{4,3,2,1,0:T(8,128)}), f32[4,2,16,32,128]{4,3,2,1,0:T(8,128)S(1)}, u32[]{:S(2)}, u32[]{:S(2)}) %all-to-all-start.1) | async-done | bytes 2097184 | tf_op jit(solution)/shard_map/all_to_all | solution.py:186
  219.4 1.3 copy-done.2
  220.7 51.3 %all_to_all.36.refs_0_ = f32[4,32,32,128]{3,2,1,0:T(8,128)S(1)} all-to-all(f32[4,32,32,128]{3,2,1,0:T(8,128)} %get-tuple-element.5), channel_id=1, replica_groups=mesh['tx'=4,'py'=2,'pz'=4] {'pz'}, dimensions={0} | all-to-all | bytes 4194304 | tf_op jit(solution)/shard_map/all_to_all | solution.py:186
  272.0 4.8 %all-to-all-start.5 = ((f32[4,32,32,128]{3,2,1,0:T(8,128)}), f32[4,32,32,128]{3,2,1,0:T(8,128)}, u32[]{:S(2)}, u32[]{:S(2)}) async-start(f32[4,32,32,128]{3,2,1,0:T(8,128)} %get-tuple-element.4), calls=%async_computation.5 | async-start | bytes 4194304 | tf_op jit(solution)/shard_map/all_to_all | solution.py:186
  276.8 1.6 dynamic-slice_bitcast_fusion.2.m_ref
  278.4 4.3 middle_refine.1.refs_0_
  284.3 22.2 %collective-permute-done.refs_1_ = f32[2,16,64,128]{3,2,1,0:T(8,128)} collective-permute-done((f32[2,16,64,128]{3,2,1,0:T(8,128)}, f32[2,16,64,128]{3,2,1,0:T(8,128)}, u32[]{:S(2)}, u32[]{:S(2)}) %collective-permute-start) | collective-permute-done | bytes 1048608 | tf_op jit(solution)/shard_map/ppermute | solution.py:190
  308.2 21.4 %collective-permute-done.2.refs_3_ = f32[2,16,64,128]{3,2,1,0:T(8,128)} collective-permute-done((f32[2,16,64,128]{3,2,1,0:T(8,128)}, f32[2,16,64,128]{3,2,1,0:T(8,128)}, u32[]{:S(2)}, u32[]{:S(2)}) %collective-permute-start.2) | collective-permute-done | bytes 1048608 | tf_op jit(solution)/shard_map/ppermute | solution.py:190
  329.7 1.1 collective-permute-start.8
  332.4 1.7 dynamic-slice_bitcast_fusion.1.m1_ref
  334.1 24.4 %contrast_last.1.c_ref = f32[2,128,64,256]{3,2,1,0:T(8,128)} custom-call(bf16[2,256,256]{2,1,0:T(8,128)(2,1)} %dynamic-slice_bitcast_fusion.1.m1_ref, bf16[2,256,512]{2,1,0:T(8,128)(2,1)} %constant.42.clone.m3_ref, f32[2,16,64,128]{3,2,1,0:T(8,128)} %middle_refine.1.refs_0_, f32[2,16,64,128]{3,2,1,0:T(8,128)} %collective-permute-done.refs_1_, ...), custom_call_target="tpu_custom_call" | custom-call | flops 12884901888 | bytes 33554432 | tf_op jit(solution)/shard_map/contrast_last/pallas_call | solution.py:165
  358.5 19.8 %collective-permute-done.8.refs_1_ = f32[4,32,32,128]{3,2,1,0:T(8,128)} collective-permute-done((f32[4,32,32,128]{3,2,1,0:T(8,128)S(1)}, f32[4,32,32,128]{3,2,1,0:T(8,128)}, u32[]{:S(2)}, u32[]{:S(2)}) %collective-permute-start.8) | collective-permute-done | bytes 2097184 | tf_op jit(solution)/shard_map/ppermute | solution.py:190
  378.3 16.1 %scatter_last.2.refs_2_ = f32[1,2,128,64,256]{4,3,2,1,0:T(8,128)} custom-call(bf16[2,256,256]{2,1,0:T(8,128)(2,1)} %dynamic-slice_bitcast_fusion.m1_ref, bf16[2,256,512]{2,1,0:T(8,128)(2,1)} %constant.41.clone.m3_ref, f32[2,128,64,256]{3,2,1,0:T(8,128)} %contrast_last.1.c_ref, f32[4,32,32,128]{3,2,1,0:T(8,128)} %copy-done, ...), custom_call_target="tpu_custom_call" | custom-call | flops 6442450944 | bytes 33554432 | tf_op jit(solution)/shard_map/scatter_last/pallas_call | solution.py:165
  394.3 28.4 %collective-permute-done.7.refs_1_ = f32[4,32,32,128]{3,2,1,0:T(8,128)} collective-permute-done((f32[4,32,32,128]{3,2,1,0:T(8,128)}, f32[4,32,32,128]{3,2,1,0:T(8,128)}, u32[]{:S(2)}, u32[]{:S(2)}) %collective-permute-start.7) | collective-permute-done | bytes 2097184 | tf_op jit(solution)/shard_map/ppermute | solution.py:190
  422.8 16.1 %scatter_last.3 = f32[1,2,128,64,256]{4,3,2,1,0:T(8,128)} custom-call(bf16[2,256,256]{2,1,0:T(8,128)(2,1)} %dynamic-slice_bitcast_fusion.m1_ref, bf16[2,256,512]{2,1,0:T(8,128)(2,1)} %constant.41.clone.m3_ref, f32[2,128,64,256]{3,2,1,0:T(8,128)} %contrast_last.1.c_ref, f32[4,32,32,128]{3,2,1,0:T(8,128)} %all-to-all-done.5.refs_0_, ...), custom_call_target="tpu_custom_call", output_to_operand_aliasing={{}: (5, {})} | custom-call | flops 6442450944 | bytes 33554432 | tf_op jit(solution)/shard_map/scatter_last/pallas_call | solution.py:165
  (23 shorter events, 7.0 us)
Async XLA Ops:
  67.5 27.8 %all-to-all-start.3 = ((f32[2,32,64,128]{3,2,1,0:T(8,128)}), f32[2,32,64,128]{3,2,1,0:T(8,128)S(1)}, u32[]{:S(2)}, u32[]{:S(2)}) async-start(f32[2,32,64,128]{3,2,1,0:T(8,128)} %middle_forward.1), calls=%async_computation.3 | async-start | bytes 4194304 | tf_op jit(solution)/shard_map/all_to_all | solution.py:186
  95.3 1.3 copy-start.1
  96.6 40.6 %all-to-all-start = ((f32[4,3,16,32,128]{4,3,2,1,0:T(8,128)}), f32[4,3,16,32,128]{4,3,2,1,0:T(8,128)S(1)}, u32[]{:S(2)}, u32[]{:S(2)}) async-start(f32[4,3,16,32,128]{4,3,2,1,0:T(8,128)} %pad_maximum_fusion), calls=%async_computation | async-start | bytes 6291456 | tf_op jit(solution)/shard_map/all_to_all | solution.py:186
  137.2 29.7 %all-to-all-start.4 = ((f32[2,32,64,128]{3,2,1,0:T(8,128)}), f32[2,32,64,128]{3,2,1,0:T(8,128)}, u32[]{:S(2)}, u32[]{:S(2)}) async-start(f32[2,32,64,128]{3,2,1,0:T(8,128)} %top_forward.1), calls=%async_computation.4 | async-start | bytes 4194304 | tf_op jit(solution)/shard_map/all_to_all | solution.py:186
  168.5 50.9 %all-to-all-start.1 = ((f32[4,2,16,32,128]{4,3,2,1,0:T(8,128)}), f32[4,2,16,32,128]{4,3,2,1,0:T(8,128)S(1)}, u32[]{:S(2)}, u32[]{:S(2)}) async-start(f32[4,2,16,32,128]{4,3,2,1,0:T(8,128)} %broadcast_in_dim.2), calls=%async_computation.1 | async-start | bytes 4194304 | tf_op jit(solution)/shard_map/all_to_all | solution.py:186
  219.4 1.3 copy-start.2
  272.0 57.7 %copy-start = (f32[4,32,32,128]{3,2,1,0:T(8,128)}, f32[4,32,32,128]{3,2,1,0:T(8,128)S(1)}, u32[]{:S(2)}) copy-start(f32[4,32,32,128]{3,2,1,0:T(8,128)S(1)} %all_to_all.36.refs_0_) | copy-start | bytes 6291460
  272.0 59.7 %copy-start.3 = (bf16[2,2,256,256]{3,2,1,0:T(8,128)(2,1)S(1)}, bf16[2,2,256,256]{3,2,1,0:T(8,128)(2,1)}, u32[]{:S(2)}) copy-start(bf16[2,2,256,256]{3,2,1,0:T(8,128)(2,1)} %constant.43.clone) | copy-start | bytes 1572868
  272.0 58.8 %all-to-all-start.5 = ((f32[4,32,32,128]{3,2,1,0:T(8,128)}), f32[4,32,32,128]{3,2,1,0:T(8,128)}, u32[]{:S(2)}, u32[]{:S(2)}) async-start(f32[4,32,32,128]{3,2,1,0:T(8,128)} %get-tuple-element.4), calls=%async_computation.5 | async-start | bytes 4194304 | tf_op jit(solution)/shard_map/all_to_all | solution.py:186
  282.6 23.9 %collective-permute-start = (f32[2,16,64,128]{3,2,1,0:T(8,128)}, f32[2,16,64,128]{3,2,1,0:T(8,128)}, u32[]{:S(2)}, u32[]{:S(2)}) collective-permute-start(f32[2,16,64,128]{3,2,1,0:T(8,128)} %middle_refine.1.refs_0_), channel_id=1, source_target_pairs={{0,4},{4,0},{1,5},{5,1},{2,6},{6,2},{3,7},{7,3},{8,12},{12,8},{9,1... | collective-permute-start | bytes 3145736 | tf_op jit(solution)/shard_map/ppermute | solution.py:190
  283.2 25.0 %collective-permute-start.1 = (f32[2,16,64,128]{3,2,1,0:T(8,128)}, f32[2,16,64,128]{3,2,1,0:T(8,128)}, u32[]{:S(2)}, u32[]{:S(2)}) collective-permute-start(f32[2,16,64,128]{3,2,1,0:T(8,128)} %middle_refine.1.refs_0_), channel_id=1, source_target_pairs={{0,16},{8,24},{16,0},{24,8},{1,17},{9,25},{17,1},{25,9},{2,18},{10... | collective-permute-start | bytes 3145736 | tf_op jit(solution)/shard_map/ppermute | solution.py:190
  306.6 23.1 %collective-permute-start.2 = (f32[2,16,64,128]{3,2,1,0:T(8,128)}, f32[2,16,64,128]{3,2,1,0:T(8,128)}, u32[]{:S(2)}, u32[]{:S(2)}) collective-permute-start(f32[2,16,64,128]{3,2,1,0:T(8,128)} %collective-permute-done.refs_1_), channel_id=1, source_target_pairs={{0,16},{8,24},{16,0},{24,8},{1,17},{9,25},{17,1},{25,9},{2,18},{10... | collective-permute-start | bytes 3145736 | tf_op jit(solution)/shard_map/ppermute | solution.py:190
  307.7 23.1 %collective-permute-start.3 = (f32[2,16,64,128]{3,2,1,0:T(8,128)}, f32[2,16,64,128]{3,2,1,0:T(8,128)}, u32[]{:S(2)}, u32[]{:S(2)}) collective-permute-start(f32[2,16,64,128]{3,2,1,0:T(8,128)} %middle_refine.1.refs_0_), channel_id=1, source_target_pairs={{0,8},{8,0},{16,24},{24,16},{1,9},{9,1},{17,25},{25,17},{2,10},{10... | collective-permute-start | bytes 3145736 | tf_op jit(solution)/shard_map/ppermute | solution.py:190
  307.7 26.4 %collective-permute-start.4 = (f32[2,16,64,128]{3,2,1,0:T(8,128)}, f32[2,16,64,128]{3,2,1,0:T(8,128)}, u32[]{:S(2)}, u32[]{:S(2)}) collective-permute-start(f32[2,16,64,128]{3,2,1,0:T(8,128)} %collective-permute-done.refs_1_), channel_id=1, source_target_pairs={{0,8},{8,0},{16,24},{24,16},{1,9},{9,1},{17,25},{25,17},{2,10},{10... | collective-permute-start | bytes 3145736 | tf_op jit(solution)/shard_map/ppermute | solution.py:190
  308.2 25.9 %collective-permute-start.5 = (f32[2,16,64,128]{3,2,1,0:T(8,128)}, f32[2,16,64,128]{3,2,1,0:T(8,128)}, u32[]{:S(2)}, u32[]{:S(2)}) collective-permute-start(f32[2,16,64,128]{3,2,1,0:T(8,128)} %collective-permute-done.1.refs_2_), channel_id=1, source_target_pairs={{0,8},{8,0},{16,24},{24,16},{1,9},{9,1},{17,25},{25,17},{2,10},{10... | collective-permute-start | bytes 3145736 | tf_op jit(solution)/shard_map/ppermute | solution.py:190
  329.7 4.4 %collective-permute-start.6 = (f32[2,16,64,128]{3,2,1,0:T(8,128)}, f32[2,16,64,128]{3,2,1,0:T(8,128)}, u32[]{:S(2)}, u32[]{:S(2)}) collective-permute-start(f32[2,16,64,128]{3,2,1,0:T(8,128)} %collective-permute-done.2.refs_3_), channel_id=1, source_target_pairs={{0,8},{8,0},{16,24},{24,16},{1,9},{9,1},{17,25},{25,17},{2,10},{10... | collective-permute-start | bytes 3145736 | tf_op jit(solution)/shard_map/ppermute | solution.py:190
  329.7 48.6 %collective-permute-start.8 = (f32[4,32,32,128]{3,2,1,0:T(8,128)S(1)}, f32[4,32,32,128]{3,2,1,0:T(8,128)}, u32[]{:S(2)}, u32[]{:S(2)}) collective-permute-start(f32[4,32,32,128]{3,2,1,0:T(8,128)S(1)} %all_to_all.36.refs_0_), channel_id=1, source_target_pairs={{0,4},{4,0},{1,5},{5,1},{2,6},{6,2},{3,7},{7,3},{8,12},{12,8},{9,1... | collective-permute-start | bytes 6291464 | tf_op jit(solution)/shard_map/ppermute | solution.py:190
  330.8 91.9 %collective-permute-start.7 = (f32[4,32,32,128]{3,2,1,0:T(8,128)}, f32[4,32,32,128]{3,2,1,0:T(8,128)}, u32[]{:S(2)}, u32[]{:S(2)}) collective-permute-start(f32[4,32,32,128]{3,2,1,0:T(8,128)} %all-to-all-done.5.refs_0_), channel_id=1, source_target_pairs={{0,4},{4,0},{1,5},{5,1},{2,6},{6,2},{3,7},{7,3},{8,12},{12,8},{9,1... | collective-permute-start | bytes 6291464 | tf_op jit(solution)/shard_map/ppermute | solution.py:190

commit v2 on v1

--- a/solution.py
+++ b/solution.py
@@ -9,6 +9,7 @@
 from jax.experimental import pallas as pl
 from jax.experimental.pallas import tpu as pltpu
 from jax.sharding import PartitionSpec as P
+
 
 F32 = jnp.float32
 BF16 = jnp.bfloat16
@@ -78,18 +79,19 @@
             o_ref[p, s] = out[p * rows : (p + 1) * rows]
 
 
-def middle_forward(m_ref, x_ref, o_ref):
-    parts, _, rows, lanes = o_ref.shape
+def middle_forward(m_ref, x_ref, *o_refs):
+    _, rows, lanes = o_refs[0].shape
     for s in range(x_ref.shape[2]):
         x = x_ref[:, :, s, :].reshape(-1, lanes)
         out = product_left(m_ref, jnp.concatenate([x, times_i(x)], axis=0), NN)
-        for p in range(parts):
-            o_ref[p, s] = out[p * rows : (p + 1) * rows]
-
-
-def top_forward(m_ref, x_ref, g_ref, o_ref):
-    parts, count, rows, lanes = x_ref.shape
-    x = jnp.concatenate([x_ref[p].reshape(count * rows, lanes) for p in range(parts)], axis=1)
+        for p, o_ref in enumerate(o_refs):
+            o_ref[s] = out[p * rows : (p + 1) * rows]
+
+
+def top_forward(parts, me_ref, m_ref, g_ref, *refs):
+    x_refs, o_refs = refs[:parts], refs[parts:]
+    count, rows, lanes = x_refs[0].shape
+    x = jnp.concatenate([r[...].reshape(count * rows, lanes) for r in x_refs], axis=1)
     v = product_right(x, m_ref)
     coarse = v.shape[1] // 2
     vr, vi = v[:, :coarse], v[:, coarse:]
@@ -97,15 +99,23 @@
     wr = vr * gr - vi * gi
     wi = vr * gi + vi * gr
     wide = coarse // parts
-    for p in range(parts):
-        cut = slice(p * wide, (p + 1) * wide)
-        o_ref[p] = jnp.concatenate([wr[:, cut], wi[:, cut]], axis=1).reshape(count, rows, lanes)
-
-
-def middle_inverse(m_ref, x_ref, *o_refs):
-    parts, _, rows, lanes = o_refs[0].shape
-    for s in range(x_ref.shape[1]):
-        x = jnp.concatenate([x_ref[p, s] for p in range(x_ref.shape[0])], axis=0)
+    blocks = [
+        jnp.concatenate([w[:, p * wide : (p + 1) * wide] for w in (wr, wi)], axis=1)
+        for p in range(parts)
+    ]
+    me = me_ref[0]
+    for j, o_ref in enumerate(o_refs):
+        picked = blocks[0]
+        for p in range(1, parts):
+            picked = jnp.where((me ^ j) == p, blocks[p], picked)
+        o_ref[...] = picked.reshape(count, rows, lanes)
+
+
+def middle_inverse(slots, m_ref, *refs):
+    x_refs, o_refs = refs[:slots], refs[slots:]
+    parts, _, rows, _ = o_refs[0].shape
+    for s in range(x_refs[0].shape[0]):
+        x = jnp.concatenate([r[s] for r in x_refs], axis=0)
         out = product_left(m_ref, jnp.concatenate([x, times_i(x)], axis=0), NN)
         for p in range(parts):
             for h, o_ref in enumerate(o_refs):
@@ -160,7 +170,7 @@
     return pl.BlockSpec(sizes, lambda i: tuple(i + offset if a == axis else 0 for a in range(len(shape))))
 
 
-def call(body, steps, in_specs, operands, shapes, out_specs, name, flops, aliases=None):
+def call(body, steps, in_specs, operands, shapes, out_specs, flops, aliases=None):
     moved = sum(math.prod(s.shape) * 4 for s in shapes) * 2
     return pl.pallas_call(
         body,
@@ -169,7 +179,6 @@
         out_specs=out_specs,
         out_shape=shapes,
         input_output_aliases=aliases or {},
-        name=name,
         cost_estimate=pl.CostEstimate(flops=flops, bytes_accessed=moved, transcendentals=0),
         compiler_params=pltpu.CompilerParams(vmem_limit_bytes=56 * 2**20),
     )(*operands)
@@ -213,9 +222,19 @@
     refine = inv @ fwd
     ri = lambda m: np.concatenate([m.real, m.imag], axis=1)
     m_fwd = jnp.asarray(halves(ri(fwd)))
-    m_inv = jnp.asarray(halves(ri(inv)))
+    order = [[y ^ j for j in range(py)] for y in range(py)]
+    rows2 = fwd.reshape(py, x1, coarse)
+    m_mid_fwd = jnp.asarray(
+        halves(np.stack([ri(rows2[o].reshape(coarse, coarse)) for o in order]))
+    )[me_y]
+    cols2 = inv.reshape(fine, py, x1)
+    m_mid_inv = jnp.asarray(
+        halves(np.stack([ri(cols2[:, o].reshape(fine, coarse)) for o in order]))
+    )[me_y]
     top = block_form(fwd).reshape(2 * coarse, 2, py, x1).transpose(2, 1, 3, 0)
-    m_top = jnp.asarray(halves(top.reshape(2 * coarse, 2 * coarse)))
+    m_top = jnp.asarray(
+        halves(np.stack([top[o].reshape(2 * coarse, 2 * coarse) for o in order]))
+    )[me_y]
     last = block_form(inv).transpose(2, 3, 0, 1).reshape(2 * coarse, 2 * fine)
     m_last = jnp.asarray(halves(last))
     last_c = block_form(refine).transpose(2, 3, 0, 1).reshape(2 * coarse, 2 * fine)
@@ -235,61 +254,65 @@
     mid = block_form(refine).reshape(2, pz, f2, 2, pz, x2).transpose(1, 0, 2, 4, 3, 5)
     m_mid = jnp.asarray(halves(mid.reshape(pz, 2 * f2, 2 * coarse)))[me_z]
 
+    spec = call(
+        depth_forward, x2 // ROWS,
+        [whole(m_fwd), pl.BlockSpec((1, 2, x1, ROWS, coarse), lambda i: (0, 0, 0, i, 0))],
+        (m_fwd, sources), [shape_of(pz, x2, k3, lanes)],
+        [along((pz, x2, k3, lanes), 1, ROWS)],
+        6 * 2 * x2 * coarse * coarse * lanes,
+    )[0]
+    spec = exchange(spec, "pz")
+
     fr, fi, sr, si = fields[:, 0], fields[:, 1], sources[:, 0], sources[:, 1]
     numer_re = jnp.sum(sr * fr + si * fi, axis=0)
     numer_im = jnp.sum(si * fr - sr * fi, axis=0)
     denom = jnp.sum(fr * fr + fi * fi, axis=0)
-    cut = lambda v: v.reshape(tx, part, x2, coarse)
-    sums = exchange(jnp.stack([cut(numer_re), cut(numer_im), cut(denom)], axis=1), "tx")
-    sums = jnp.sum(sums, axis=0)
-    contrast = sums[:2] / sums[2:]
-
-    spec = call(
-        depth_forward, x2 // ROWS,
-        [whole(m_fwd), pl.BlockSpec((1, 2, x1, ROWS, coarse), lambda i: (0, 0, 0, i, 0))],
-        (m_fwd, sources), [shape_of(pz, x2, k3, lanes)], [along((pz, x2, k3, lanes), 1, ROWS)],
-        "depth_forward", 6 * 2 * x2 * coarse * coarse * lanes,
-    )[0]
-    spec = exchange(spec, "pz")
-    spec = call(
+    sums = jnp.stack([numer_re, numer_im, denom])
+    blocks = [lax.dynamic_slice_in_dim(sums, (me_x ^ j) * part, part, axis=1) for j in range(tx)]
+    blocks = [blocks[0]] + [swap(blocks[j], "tx", tx, j) for j in range(1, tx)]
+    total = functools.reduce(jnp.add, blocks)
+    contrast = total[:2] / total[2:]
+    spread = jnp.broadcast_to(contrast[None], (pz,) + contrast.shape)
+    seen = exchange(spread, "pz")
+
+    slab = (k3, x1, lanes)
+    specs = call(
         middle_forward, k3 // ROWS,
-        [whole(m_fwd), along(spec.shape, 2, ROWS)],
-        (m_fwd, spec), [shape_of(py, k3, x1, lanes)], [along((py, k3, x1, lanes), 1, ROWS)],
-        "middle_forward", 6 * 2 * k3 * coarse * coarse * lanes,
-    )[0]
-    spec = exchange(spec, "py")
-    spec = call(
-        top_forward, k3 // ROWS,
-        [whole(m_top), along(spec.shape, 1, ROWS), along(green.shape, 1, ROWS)],
-        (m_top, spec, green), [shape_of(py, k3, x1, lanes)], [along((py, k3, x1, lanes), 1, ROWS)],
-        "top_forward", 6 * 4 * k3 * x1 * coarse * coarse,
-    )[0]
-    spec = exchange(spec, "py")
+        [whole(m_mid_fwd), along(spec.shape, 2, ROWS)],
+        (m_mid_fwd, spec), [shape_of(*slab)] * py, [along(slab, 0, ROWS)] * py,
+        6 * 2 * k3 * coarse * coarse * lanes,
+    )
+    specs = [specs[0]] + [swap(specs[j], "py", py, j) for j in range(1, py)]
+    specs = call(
+        functools.partial(top_forward, py), k3 // ROWS,
+        [pl.BlockSpec(memory_space=pltpu.SMEM), whole(m_top), along(green.shape, 1, ROWS)]
+        + [along(slab, 0, ROWS)] * py,
+        (me_y.reshape(1), m_top, green, *specs),
+        [shape_of(*slab)] * py, [along(slab, 0, ROWS)] * py,
+        6 * 4 * k3 * x1 * coarse * coarse,
+    )
+    specs = [specs[0]] + [swap(specs[j], "py", py, j) for j in range(1, py)]
 
     some = f2 // chunks
     dims = (pz, k3, some, lanes)
     pieces = call(
-        middle_inverse, k3 // ROWS,
-        [whole(m_inv), along(spec.shape, 1, ROWS)],
-        (m_inv, spec), [shape_of(*dims)] * chunks, [along(dims, 1, ROWS)] * chunks,
-        "middle_inverse", 6 * 2 * k3 * fine * coarse * lanes,
-    )
-
-    spread = jnp.broadcast_to(contrast[None], (pz,) + contrast.shape)
-    seen = exchange(spread, "pz")
+        functools.partial(middle_inverse, py), k3 // ROWS,
+        [whole(m_mid_inv)] + [along(slab, 0, ROWS)] * py,
+        (m_mid_inv, *specs), [shape_of(*dims)] * chunks, [along(dims, 1, ROWS)] * chunks,
+        6 * 2 * k3 * fine * coarse * lanes,
+    )
+
     ref_dims = (2, part, f2, coarse)
     step = min(4, part)
     mine = call(
         middle_refine, part // step,
         [whole(m_mid), along(seen.shape, 2, step)],
         (m_mid, seen), [shape_of(*ref_dims)], [along(ref_dims, 1, step)],
-        "middle_refine", 6 * 4 * part * f2 * coarse * coarse,
+        6 * 4 * part * f2 * coarse * coarse,
     )[0]
-    slots = []
-    for j, piece in gather_slots([mine], "py", py):
-        slots += [(j, piece)]
-    order, parts = [s[0] for s in slots], [s[1] for s in slots]
-    bit, codes = tx // 2, [(j, 0) for j in order]
+    slots = gather_slots([mine], "py", py)
+    parts = [p for _, p in slots]
+    bit, codes = tx // 2, [(j, 0) for j, _ in slots]
     while bit:
         parts = parts + [swap(p, "tx", tx, bit) for p in parts]
         codes = codes + [(j, t | bit) for j, t in codes]
@@ -310,7 +333,7 @@
         contrast_last, f2 // ROWS,
         [whole(m_first_c), whole(m_last_c)] + [along(ref_dims, 2, ROWS)] * len(parts),
         (m_first_c, m_last_c, *parts), [shape_of(*out_dims)], [along(out_dims, 2, ROWS)],
-        "contrast_last", 6 * 8 * f1 * f2 * coarse * fine,
+        6 * 8 * f1 * f2 * coarse * fine,
     )[0]
 
     scattered = None
@@ -330,7 +353,7 @@
         scattered = call(
             functools.partial(scatter_last, py), some // ROWS, specs, operands,
             [shape_of(*scat_dims)], [along(scat_dims, 3, ROWS, offset)],
-            "scatter_last", 6 * 8 * f1 * some * coarse * fine, aliases,
+            6 * 8 * f1 * some * coarse * fine, aliases,
         )[0]
     return contrast_fine, scattered
 
@@ -398,7 +421,7 @@
 
 def solution(mesh):
     tx, py, pz = mesh.shape["tx"], mesh.shape["py"], mesh.shape["pz"]
-    chunks = 2
+    chunks = 4
 
     def on_device(fields, sources, green):
         x1, x2, coarse = fields.shape[2:]

time: 440 us -> 360 us (0.82)
  blocking collectives: 106 us -> 28.8 us
  waiting for transfers between devices: 200 us -> 176 us
  starting transfers between devices: 26 us -> 37.8 us
  Pallas kernels: 84.9 us -> 92 us
  local copies, waits for them, and re-layouts: 9.15 us -> 14.1 us
    all_to_all x5, waiting for transfers between devices: 109 us -> 23.5 us  [exchange(): return lax.all_to_all(x, axis, 0, 0, tiled=True)]
    all_to_all x2 -> x1, blocking collectives: 106 us -> 28.8 us  [exchange(): return lax.all_to_all(x, axis, 0, 0, tiled=True)]
    ppermute x9 -> x16, waiting for transfers between devices: 91.9 us -> 153 us  [swap(): return lax.ppermute(x, axis, [(i, i ^ bit) for i in range(size)])]
    ppermute x9 -> x16, starting transfers between devices: 5.37 us -> 14.2 us  [swap(): return lax.ppermute(x, axis, [(i, i ^ bit) for i in range(size)])]
    pallas_call x8 -> x10, Pallas kernels: 84.9 us -> 92 us  [call(): pl.pallas_call(body, grid=(steps,), in_specs=in_specs, out_specs=out_spec...]
  transfers between devices with their start and end apart: 14 -> 21, of which waited for: 8 -> 12; matrix products, arithmetic and copies ran while one was open for 4% -> 5% of each run, Pallas kernels for 13% -> 21%
where the time goes in v2:
time: 360 us; the launch traced here: 359 us
  waiting for transfers between devices  176 us (49%)
  Pallas kernels  92 us (26%)
  starting transfers between devices  37.8 us (10%)
  blocking collectives  28.8 us (8%)
  local copies, waits for them, and re-layouts  14.1 us (4%)
  other arithmetic  9.64 us (3%)
    ppermute x16, waiting for transfers between devices, swap(): return lax.ppermute(x, axis, [(i, i ^ bit) for i in range(size)])  153 us
    pallas_call x10, Pallas kernels, call(): pl.pallas_call(body, grid=(steps,), in_specs=in_specs, out_specs=out_spec...  92 us
    all_to_all x1, blocking collectives, exchange(): return lax.all_to_all(x, axis, 0, 0, tiled=True)  28.8 us
    all_to_all x5, starting transfers between devices, exchange(): return lax.all_to_all(x, axis, 0, 0, tiled=True)  23.6 us
    all_to_all x5, waiting for transfers between devices, exchange(): return lax.all_to_all(x, axis, 0, 0, tiled=True)  23.5 us
    ppermute x16, starting transfers between devices, swap(): return lax.ppermute(x, axis, [(i, i ^ bit) for i in range(size)])  14.2 us
    reduce_sum x1, other arithmetic, aligned_device(): numer_re = jnp.sum(sr * fr + si * fi, axis=0)  7.31 us
  transfers between devices with their start and end apart: 21, of which 12 were waited for; matrix products, arithmetic and copies ran while one was open for 5% of the time, Pallas kernels for 21%

profile of v2, /device:TPU:0, one launch (start us, length us, event | category | flops | bytes accessed | tf_op | source)
XLA Modules:
  0.0 359.1 jit_solution(1642267482992163659)
XLA Ops:
  0.6 5.8 %shard_map.133 = f32[4,32,32,128]{3,2,1,0:T(8,128)} custom-call(bf16[2,128,256]{2,1,0:T(8,128)(2,1)} %constant.48.clone.m_ref, f32[4,2,64,32,128]{4,3,2,1,0:T(8,128)} %x_ref.1), custom_call_target="tpu_custom_call" | custom-call | flops 805306368 | bytes 4194304 | tf_op jit(solution)/shard_map/pallas_call | solution.py:175
  6.4 6.3 %all-to-all-start.1 = ((f32[4,32,32,128]{3,2,1,0:T(8,128)}), f32[4,32,32,128]{3,2,1,0:T(8,128)}, u32[]{:S(2)}, u32[]{:S(2)}) async-start(f32[4,32,32,128]{3,2,1,0:T(8,128)} %shard_map.133), calls=%async_computation.1 | async-start | bytes 4194304 | tf_op jit(solution)/shard_map/all_to_all | solution.py:195
  12.8 7.3 %add_reduce_fusion.1 = (f32[64,32,128]{2,1,0:T(8,128)S(1)}, f32[64,32,128]{2,1,0:T(8,128)S(1)}, f32[64,32,128]{2,1,0:T(8,128)S(1)}) fusion(f32[4,2,64,32,128]{4,3,2,1,0:T(8,128)} %x_ref.1, f32[4,2,64,32,128]{4,3,2,1,0:T(8,128)} %param.12), kind=kLoop, calls=%fused_computation.2 | loop fusion | flops 11796480 | bytes 19922944 | tf_op jit(solution)/shard_map/reduce_sum | solution.py:267
  24.5 18.1 %collective-permute-done.1 = f32[3,16,32,128]{3,2,1,0:T(8,128)} collective-permute-done((f32[3,16,32,128]{3,2,1,0:T(8,128)}, f32[3,16,32,128]{3,2,1,0:T(8,128)}, u32[]{:S(2)}, u32[]{:S(2)}) %collective-permute-start.1) | collective-permute-done | bytes 786464 | tf_op jit(solution)/shard_map/ppermute | solution.py:199
  42.6 15.9 %collective-permute-done.2 = f32[3,16,32,128]{3,2,1,0:T(8,128)} collective-permute-done((f32[3,16,32,128]{3,2,1,0:T(8,128)}, f32[3,16,32,128]{3,2,1,0:T(8,128)}, u32[]{:S(2)}, u32[]{:S(2)}) %collective-permute-start.2) | collective-permute-done | bytes 786464 | tf_op jit(solution)/shard_map/ppermute | solution.py:199
  58.5 2.0 add_add_fusion
  61.1 1.6 broadcast_in_dim.2
  62.6 4.8 %all-to-all-start = ((f32[4,2,16,32,128]{4,3,2,1,0:T(8,128)}), f32[4,2,16,32,128]{4,3,2,1,0:T(8,128)S(1)}, u32[]{:S(2)}, u32[]{:S(2)}) async-start(f32[4,2,16,32,128]{4,3,2,1,0:T(8,128)} %broadcast_in_dim.2), calls=%async_computation | async-start | bytes 4194304 | tf_op jit(solution)/shard_map/all_to_all | solution.py:195
  68.1 6.4 %shard_map.134 = (f32[32,64,128]{2,1,0:T(8,128)}, f32[32,64,128]{2,1,0:T(8,128)}) custom-call(bf16[2,128,256]{2,1,0:T(8,128)(2,1)} %dynamic-slice_bitcast_fusion.4.m_ref, f32[4,32,32,128]{3,2,1,0:T(8,128)} %all-to-all-done.1.x_ref), custom_call_target="tpu_custom_call" | custom-call | flops 805306368 | bytes 4194304 | tf_op jit(solution)/shard_map/pallas_call | solution.py:175
  76.7 23.0 %collective-permute-done.10.refs_1_ = f32[32,64,128]{2,1,0:T(8,128)S(1)} collective-permute-done((f32[32,64,128]{2,1,0:T(8,128)}, f32[32,64,128]{2,1,0:T(8,128)S(1)}, u32[]{:S(2)}, u32[]{:S(2)}) %collective-permute-start.10) | collective-permute-done | bytes 1048608 | tf_op jit(solution)/shard_map/ppermute | solution.py:199
  100.7 5.1 %shard_map.135 = (f32[32,64,128]{2,1,0:T(8,128)}, f32[32,64,128]{2,1,0:T(8,128)}) custom-call(s32[1]{0:T(128)} %bitcast.8.me_ref, bf16[2,256,256]{2,1,0:T(8,128)(2,1)} %dynamic-slice_bitcast_fusion.m_ref, f32[2,32,64,128]{3,2,1,0:T(8,128)} %g_ref.1, f32[32,64,128]{2,1,0:T(8,128)} %get-tuple-element.10.refs_0_, f32[32,64,128]{2,1,0:T(8,128)} %copy-done.5), custom_call_target="tpu_custom_call" | custom-call | flops 805306368 | bytes 4194304 | tf_op jit(solution)/shard_map/pallas_call | solution.py:175
  108.1 22.2 %collective-permute-done.11.refs_1_ = f32[32,64,128]{2,1,0:T(8,128)S(1)} collective-permute-done((f32[32,64,128]{2,1,0:T(8,128)}, f32[32,64,128]{2,1,0:T(8,128)S(1)}, u32[]{:S(2)}, u32[]{:S(2)}) %collective-permute-start.11) | collective-permute-done | bytes 1048608 | tf_op jit(solution)/shard_map/ppermute | solution.py:199
  131.2 6.8 %shard_map.136 = (f32[4,32,16,128]{3,2,1,0:T(8,128)}, f32[4,32,16,128]{3,2,1,0:T(8,128)}, f32[4,32,16,128]{3,2,1,0:T(8,128)}, f32[4,32,16,128]{3,2,1,0:T(8,128)}) custom-call(bf16[2,256,256]{2,1,0:T(8,128)(2,1)} %dynamic-slice_bitcast_fusion.1.m_ref, f32[32,64,128]{2,1,0:T(8,128)} %get-tuple-element.12.refs_0_, f32[32,64,128]{2,1,0:T(8,128)} %copy-done.9), custom_call_target="tpu_custom_call" | custom-call | flops 1610612736 | bytes 8388608 | tf_op jit(solution)/shard_map/pallas_call | solution.py:175
  138.0 28.8 %all_to_all.30.refs_0_ = f32[4,32,16,128]{3,2,1,0:T(8,128)} all-to-all(f32[4,32,16,128]{3,2,1,0:T(8,128)} %get-tuple-element.17), channel_id=1, replica_groups=mesh['tx'=4,'py'=2,'pz'=4] {'pz'}, dimensions={0} | all-to-all | bytes 2097152 | tf_op jit(solution)/shard_map/all_to_all | solution.py:195
  166.8 3.5 all-to-all-start.4
  170.3 1.6 dynamic-slice_bitcast_fusion.5.m_ref
  171.9 23.1 %all-to-all-done.4.refs_0_ = f32[4,32,16,128]{3,2,1,0:T(8,128)S(1)} async-done(((f32[4,32,16,128]{3,2,1,0:T(8,128)}), f32[4,32,16,128]{3,2,1,0:T(8,128)S(1)}, u32[]{:S(2)}, u32[]{:S(2)}) %all-to-all-start.4) | async-done | bytes 1048608 | tf_op jit(solution)/shard_map/all_to_all | solution.py:195
  195.0 4.2 %all-to-all-start.3 = ((f32[4,32,16,128]{3,2,1,0:T(8,128)}), f32[4,32,16,128]{3,2,1,0:T(8,128)}, u32[]{:S(2)}, u32[]{:S(2)}) async-start(f32[4,32,16,128]{3,2,1,0:T(8,128)} %get-tuple-element.15), calls=%async_computation.3 | async-start | bytes 2097152 | tf_op jit(solution)/shard_map/all_to_all | solution.py:195
  199.2 4.3 %shard_map.131.refs_0_ = f32[2,16,64,128]{3,2,1,0:T(8,128)} custom-call(bf16[2,128,256]{2,1,0:T(8,128)(2,1)} %dynamic-slice_bitcast_fusion.5.m_ref, f32[4,2,16,32,128]{4,3,2,1,0:T(8,128)} %copy-done), custom_call_target="tpu_custom_call" | custom-call | flops 402653184 | bytes 2097152 | tf_op jit(solution)/shard_map/pallas_call | solution.py:175
  206.6 21.5 %collective-permute-done.3.refs_1_ = f32[2,16,64,128]{3,2,1,0:T(8,128)} collective-permute-done((f32[2,16,64,128]{3,2,1,0:T(8,128)}, f32[2,16,64,128]{3,2,1,0:T(8,128)}, u32[]{:S(2)}, u32[]{:S(2)}) %collective-permute-start.3) | collective-permute-done | bytes 1048608 | tf_op jit(solution)/shard_map/ppermute | solution.py:199
  229.5 4.7 %all-to-all-start.2 = ((f32[4,32,16,128]{3,2,1,0:T(8,128)}), f32[4,32,16,128]{3,2,1,0:T(8,128)S(1)}, u32[]{:S(2)}, u32[]{:S(2)}) async-start(f32[4,32,16,128]{3,2,1,0:T(8,128)} %get-tuple-element.14), calls=%async_computation.2 | async-start | bytes 2097152 | tf_op jit(solution)/shard_map/all_to_all | solution.py:195
  234.8 17.0 %collective-permute-done.5.refs_3_ = f32[2,16,64,128]{3,2,1,0:T(8,128)} collective-permute-done((f32[2,16,64,128]{3,2,1,0:T(8,128)}, f32[2,16,64,128]{3,2,1,0:T(8,128)}, u32[]{:S(2)}, u32[]{:S(2)}) %collective-permute-start.5) | collective-permute-done | bytes 1048608 | tf_op jit(solution)/shard_map/ppermute | solution.py:199
  251.8 1.7 dynamic-slice_bitcast_fusion.2.m1_ref
  253.5 1.7 dynamic-slice_bitcast_fusion.3.m1_ref
  259.4 24.4 %shard_map.132.c_ref = f32[2,128,64,256]{3,2,1,0:T(8,128)} custom-call(bf16[2,256,256]{2,1,0:T(8,128)(2,1)} %dynamic-slice_bitcast_fusion.3.m1_ref, bf16[2,256,512]{2,1,0:T(8,128)(2,1)} %constant.53.clone.m3_ref, f32[2,16,64,128]{3,2,1,0:T(8,128)} %shard_map.131.refs_0_, f32[2,16,64,128]{3,2,1,0:T(8,128)} %collective-permute-done.3.refs_1_, ...), custom_call_target="tpu_custom_call" | custom-call | flops 12884901888 | bytes 33554432 | tf_op jit(solution)/shard_map/pallas_call | solution.py:175
  284.8 9.8 %shard_map.137.refs_2_ = f32[1,2,128,64,256]{4,3,2,1,0:T(8,128)} custom-call(bf16[2,256,256]{2,1,0:T(8,128)(2,1)} %dynamic-slice_bitcast_fusion.2.m1_ref, bf16[2,256,512]{2,1,0:T(8,128)(2,1)} %constant.52.clone.m3_ref, f32[2,128,64,256]{3,2,1,0:T(8,128)} %shard_map.132.c_ref, f32[4,32,16,128]{3,2,1,0:T(8,128)} %all_to_all.30.refs_0_, ...), custom_call_target="tpu_custom_call" | custom-call | flops 3221225472 | bytes 33554432 | tf_op jit(solution)/shard_map/pallas_call | solution.py:175
  294.6 9.3 %collective-permute-done.14.refs_1_ = f32[4,32,16,128]{3,2,1,0:T(8,128)} collective-permute-done((f32[4,32,16,128]{3,2,1,0:T(8,128)S(1)}, f32[4,32,16,128]{3,2,1,0:T(8,128)}, u32[]{:S(2)}, u32[]{:S(2)}) %collective-permute-start.14) | collective-permute-done | bytes 1048608 | tf_op jit(solution)/shard_map/ppermute | solution.py:199
  303.9 9.8 %shard_map.138.refs_2_ = f32[1,2,128,64,256]{4,3,2,1,0:T(8,128)} custom-call(bf16[2,256,256]{2,1,0:T(8,128)(2,1)} %dynamic-slice_bitcast_fusion.2.m1_ref, bf16[2,256,512]{2,1,0:T(8,128)(2,1)} %constant.52.clone.m3_ref, f32[2,128,64,256]{3,2,1,0:T(8,128)} %shard_map.132.c_ref, f32[4,32,16,128]{3,2,1,0:T(8,128)} %copy-done.1, ...), custom_call_target="tpu_custom_call", output_to_operand_aliasing={{}: (5, {})} | custom-call | flops 3221225472 | bytes 33554432 | tf_op jit(solution)/shard_map/pallas_call | solution.py:175
  313.7 12.7 %collective-permute-done.13.refs_1_ = f32[4,32,16,128]{3,2,1,0:T(8,128)} collective-permute-done((f32[4,32,16,128]{3,2,1,0:T(8,128)}, f32[4,32,16,128]{3,2,1,0:T(8,128)}, u32[]{:S(2)}, u32[]{:S(2)}) %collective-permute-start.13) | collective-permute-done | bytes 1048608 | tf_op jit(solution)/shard_map/ppermute | solution.py:199
  326.4 9.8 %shard_map.139.refs_2_ = f32[1,2,128,64,256]{4,3,2,1,0:T(8,128)} custom-call(bf16[2,256,256]{2,1,0:T(8,128)(2,1)} %dynamic-slice_bitcast_fusion.2.m1_ref, bf16[2,256,512]{2,1,0:T(8,128)(2,1)} %constant.52.clone.m3_ref, f32[2,128,64,256]{3,2,1,0:T(8,128)} %shard_map.132.c_ref, ...), custom_call_target="tpu_custom_call", output_to_operand_aliasing={{}: (5, {})} | custom-call | flops 3221225472 | bytes 33554432 | tf_op jit(solution)/shard_map/pallas_call | solution.py:175
  336.2 12.1 %collective-permute-done.12.refs_1_ = f32[4,32,16,128]{3,2,1,0:T(8,128)S(1)} collective-permute-done((f32[4,32,16,128]{3,2,1,0:T(8,128)S(1)}, f32[4,32,16,128]{3,2,1,0:T(8,128)S(1)}, u32[]{:S(2)}, u32[]{:S(2)}) %collective-permute-start.12) | collective-permute-done | bytes 1048608 | tf_op jit(solution)/shard_map/ppermute | solution.py:199
  349.3 9.8 %shard_map.140 = f32[1,2,128,64,256]{4,3,2,1,0:T(8,128)} custom-call(bf16[2,256,256]{2,1,0:T(8,128)(2,1)} %dynamic-slice_bitcast_fusion.2.m1_ref, bf16[2,256,512]{2,1,0:T(8,128)(2,1)} %constant.52.clone.m3_ref, f32[2,128,64,256]{3,2,1,0:T(8,128)} %shard_map.132.c_ref, f32[4,32,16,128]{3,2,1,0:T(8,128)} %copy-done.2, ...), custom_call_target="tpu_custom_call", output_to_operand_aliasing={{}: (5, {})} | custom-call | flops 3221225472 | bytes 33554432 | tf_op jit(solution)/shard_map/pallas_call | solution.py:175
  (54 shorter events, 23.4 us)
Async XLA Ops:
  6.4 54.7 %all-to-all-start.1 = ((f32[4,32,32,128]{3,2,1,0:T(8,128)}), f32[4,32,32,128]{3,2,1,0:T(8,128)}, u32[]{:S(2)}, u32[]{:S(2)}) async-start(f32[4,32,32,128]{3,2,1,0:T(8,128)} %shard_map.133), calls=%async_computation.1 | async-start | bytes 4194304 | tf_op jit(solution)/shard_map/all_to_all | solution.py:195
  21.9 2.6 collective-permute-start
  21.9 20.7 %collective-permute-start.1 = (f32[3,16,32,128]{3,2,1,0:T(8,128)}, f32[3,16,32,128]{3,2,1,0:T(8,128)}, u32[]{:S(2)}, u32[]{:S(2)}) collective-permute-start(f32[3,16,32,128]{3,2,1,0:T(8,128)} %get-tuple-element.23), channel_id=1, source_target_pairs={{0,16},{8,24},{16,0},{24,8},{1,17},{9,25},{17,1},{25,9},{2,18},{10... | collective-permute-start | bytes 2359304 | tf_op jit(solution)/shard_map/ppermute | solution.py:199
  23.4 35.2 %collective-permute-start.2 = (f32[3,16,32,128]{3,2,1,0:T(8,128)}, f32[3,16,32,128]{3,2,1,0:T(8,128)}, u32[]{:S(2)}, u32[]{:S(2)}) collective-permute-start(f32[3,16,32,128]{3,2,1,0:T(8,128)} %get-tuple-element.22), channel_id=1, source_target_pairs={{0,24},{8,16},{16,8},{24,0},{1,25},{9,17},{17,9},{25,1},{2,26},{10... | collective-permute-start | bytes 2359304 | tf_op jit(solution)/shard_map/ppermute | solution.py:199
  60.5 6.9 %copy-start.8 = (bf16[2,2,128,256]{3,2,1,0:T(8,128)(2,1)S(1)}, bf16[2,2,128,256]{3,2,1,0:T(8,128)(2,1)}, u32[]{:S(2)}) copy-start(bf16[2,2,128,256]{3,2,1,0:T(8,128)(2,1)} %constant.49.clone) | copy-start | bytes 786436
  62.6 13.4 %copy-start.7 = (bf16[2,2,256,256]{3,2,1,0:T(8,128)(2,1)S(1)}, bf16[2,2,256,256]{3,2,1,0:T(8,128)(2,1)}, u32[]{:S(2)}) copy-start(bf16[2,2,256,256]{3,2,1,0:T(8,128)(2,1)} %constant.51.clone) | copy-start | bytes 1572868
  62.6 75.4 %all-to-all-start = ((f32[4,2,16,32,128]{4,3,2,1,0:T(8,128)}), f32[4,2,16,32,128]{4,3,2,1,0:T(8,128)S(1)}, u32[]{:S(2)}, u32[]{:S(2)}) async-start(f32[4,2,16,32,128]{4,3,2,1,0:T(8,128)} %broadcast_in_dim.2), calls=%async_computation | async-start | bytes 4194304 | tf_op jit(solution)/shard_map/all_to_all | solution.py:195
  67.4 39.9 %copy-start.6 = (bf16[2,2,256,256]{3,2,1,0:T(8,128)(2,1)S(1)}, bf16[2,2,256,256]{3,2,1,0:T(8,128)(2,1)}, u32[]{:S(2)}) copy-start(bf16[2,2,256,256]{3,2,1,0:T(8,128)(2,1)} %constant.50.clone) | copy-start | bytes 1572868
  74.5 25.3 %collective-permute-start.10 = (f32[32,64,128]{2,1,0:T(8,128)}, f32[32,64,128]{2,1,0:T(8,128)S(1)}, u32[]{:S(2)}, u32[]{:S(2)}) collective-permute-start(f32[32,64,128]{2,1,0:T(8,128)} %get-tuple-element.11), channel_id=1, source_target_pairs={{0,4},{4,0},{1,5},{5,1},{2,6},{6,2},{3,7},{7,3},{8,12},{12,8},{9,1... | collective-permute-start | bytes 3145736 | tf_op jit(solution)/shard_map/ppermute | solution.py:199
  99.8 1.0 copy-start.5
  105.8 24.4 %collective-permute-start.11 = (f32[32,64,128]{2,1,0:T(8,128)}, f32[32,64,128]{2,1,0:T(8,128)S(1)}, u32[]{:S(2)}, u32[]{:S(2)}) collective-permute-start(f32[32,64,128]{2,1,0:T(8,128)} %get-tuple-element.13), channel_id=1, source_target_pairs={{0,4},{4,0},{1,5},{5,1},{2,6},{6,2},{3,7},{7,3},{8,12},{12,8},{9,1... | collective-permute-start | bytes 3145736 | tf_op jit(solution)/shard_map/ppermute | solution.py:199
  130.2 1.0 copy-start.9
  138.0 61.2 %copy-start = (f32[4,2,16,32,128]{4,3,2,1,0:T(8,128)}, f32[4,2,16,32,128]{4,3,2,1,0:T(8,128)S(1)}, u32[]{:S(2)}) copy-start(f32[4,2,16,32,128]{4,3,2,1,0:T(8,128)S(1)} %all-to-all-done.x_ref) | copy-start | bytes 6291460
  166.8 28.2 %all-to-all-start.4 = ((f32[4,32,16,128]{3,2,1,0:T(8,128)}), f32[4,32,16,128]{3,2,1,0:T(8,128)S(1)}, u32[]{:S(2)}, u32[]{:S(2)}) async-start(f32[4,32,16,128]{3,2,1,0:T(8,128)} %get-tuple-element.16), calls=%async_computation.4 | async-start | bytes 2097152 | tf_op jit(solution)/shard_map/all_to_all | solution.py:195
  195.0 61.6 %copy-start.1 = (f32[4,32,16,128]{3,2,1,0:T(8,128)}, f32[4,32,16,128]{3,2,1,0:T(8,128)S(1)}, u32[]{:S(2)}) copy-start(f32[4,32,16,128]{3,2,1,0:T(8,128)S(1)} %all-to-all-done.4.refs_0_) | copy-start | bytes 3145732
  195.0 34.6 %all-to-all-start.3 = ((f32[4,32,16,128]{3,2,1,0:T(8,128)}), f32[4,32,16,128]{3,2,1,0:T(8,128)}, u32[]{:S(2)}, u32[]{:S(2)}) async-start(f32[4,32,16,128]{3,2,1,0:T(8,128)} %get-tuple-element.15), calls=%async_computation.3 | async-start | bytes 2097152 | tf_op jit(solution)/shard_map/all_to_all | solution.py:195
  203.6 24.5 %collective-permute-start.3 = (f32[2,16,64,128]{3,2,1,0:T(8,128)}, f32[2,16,64,128]{3,2,1,0:T(8,128)}, u32[]{:S(2)}, u32[]{:S(2)}) collective-permute-start(f32[2,16,64,128]{3,2,1,0:T(8,128)} %shard_map.131.refs_0_), channel_id=1, source_target_pairs={{0,4},{4,0},{1,5},{5,1},{2,6},{6,2},{3,7},{7,3},{8,12},{12,8},{9,1... | collective-permute-start | bytes 3145736 | tf_op jit(solution)/shard_map/ppermute | solution.py:199
  205.1 29.7 %collective-permute-start.4 = (f32[2,16,64,128]{3,2,1,0:T(8,128)}, f32[2,16,64,128]{3,2,1,0:T(8,128)}, u32[]{:S(2)}, u32[]{:S(2)}) collective-permute-start(f32[2,16,64,128]{3,2,1,0:T(8,128)} %shard_map.131.refs_0_), channel_id=1, source_target_pairs={{0,16},{8,24},{16,0},{24,8},{1,17},{9,25},{17,1},{25,9},{2,18},{10... | collective-permute-start | bytes 3145736 | tf_op jit(solution)/shard_map/ppermute | solution.py:199
  228.1 23.7 %collective-permute-start.5 = (f32[2,16,64,128]{3,2,1,0:T(8,128)}, f32[2,16,64,128]{3,2,1,0:T(8,128)}, u32[]{:S(2)}, u32[]{:S(2)}) collective-permute-start(f32[2,16,64,128]{3,2,1,0:T(8,128)} %collective-permute-done.3.refs_1_), channel_id=1, source_target_pairs={{0,16},{8,24},{16,0},{24,8},{1,17},{9,25},{17,1},{25,9},{2,18},{10... | collective-permute-start | bytes 3145736 | tf_op jit(solution)/shard_map/ppermute | solution.py:199
  229.5 29.1 %all-to-all-start.2 = ((f32[4,32,16,128]{3,2,1,0:T(8,128)}), f32[4,32,16,128]{3,2,1,0:T(8,128)S(1)}, u32[]{:S(2)}, u32[]{:S(2)}) async-start(f32[4,32,16,128]{3,2,1,0:T(8,128)} %get-tuple-element.14), calls=%async_computation.2 | async-start | bytes 2097152 | tf_op jit(solution)/shard_map/all_to_all | solution.py:195
  234.3 22.3 %collective-permute-start.6 = (f32[2,16,64,128]{3,2,1,0:T(8,128)}, f32[2,16,64,128]{3,2,1,0:T(8,128)}, u32[]{:S(2)}, u32[]{:S(2)}) collective-permute-start(f32[2,16,64,128]{3,2,1,0:T(8,128)} %shard_map.131.refs_0_), channel_id=1, source_target_pairs={{0,8},{8,0},{16,24},{24,16},{1,9},{9,1},{17,25},{25,17},{2,10},{10... | collective-permute-start | bytes 3145736 | tf_op jit(solution)/shard_map/ppermute | solution.py:199
  234.3 22.9 %collective-permute-start.7 = (f32[2,16,64,128]{3,2,1,0:T(8,128)}, f32[2,16,64,128]{3,2,1,0:T(8,128)}, u32[]{:S(2)}, u32[]{:S(2)}) collective-permute-start(f32[2,16,64,128]{3,2,1,0:T(8,128)} %collective-permute-done.3.refs_1_), channel_id=1, source_target_pairs={{0,8},{8,0},{16,24},{24,16},{1,9},{9,1},{17,25},{25,17},{2,10},{10... | collective-permute-start | bytes 3145736 | tf_op jit(solution)/shard_map/ppermute | solution.py:199
  234.8 23.8 %collective-permute-start.8 = (f32[2,16,64,128]{3,2,1,0:T(8,128)}, f32[2,16,64,128]{3,2,1,0:T(8,128)}, u32[]{:S(2)}, u32[]{:S(2)}) collective-permute-start(f32[2,16,64,128]{3,2,1,0:T(8,128)} %collective-permute-done.4.refs_2_), channel_id=1, source_target_pairs={{0,8},{8,0},{16,24},{24,16},{1,9},{9,1},{17,25},{25,17},{2,10},{10... | collective-permute-start | bytes 3145736 | tf_op jit(solution)/shard_map/ppermute | solution.py:199
  251.8 7.6 %collective-permute-start.9 = (f32[2,16,64,128]{3,2,1,0:T(8,128)}, f32[2,16,64,128]{3,2,1,0:T(8,128)}, u32[]{:S(2)}, u32[]{:S(2)}) collective-permute-start(f32[2,16,64,128]{3,2,1,0:T(8,128)} %collective-permute-done.5.refs_3_), channel_id=1, source_target_pairs={{0,8},{8,0},{16,24},{24,16},{1,9},{9,1},{17,25},{25,17},{2,10},{10... | collective-permute-start | bytes 3145736 | tf_op jit(solution)/shard_map/ppermute | solution.py:199
  255.1 28.7 %collective-permute-start.15 = (f32[4,32,16,128]{3,2,1,0:T(8,128)}, f32[4,32,16,128]{3,2,1,0:T(8,128)S(1)}, u32[]{:S(2)}, u32[]{:S(2)}) collective-permute-start(f32[4,32,16,128]{3,2,1,0:T(8,128)} %all_to_all.30.refs_0_), channel_id=1, source_target_pairs={{0,4},{4,0},{1,5},{5,1},{2,6},{6,2},{3,7},{7,3},{8,12},{12,8},{9,1... | collective-permute-start | bytes 3145736 | tf_op jit(solution)/shard_map/ppermute | solution.py:199
  256.6 47.4 %collective-permute-start.14 = (f32[4,32,16,128]{3,2,1,0:T(8,128)S(1)}, f32[4,32,16,128]{3,2,1,0:T(8,128)}, u32[]{:S(2)}, u32[]{:S(2)}) collective-permute-start(f32[4,32,16,128]{3,2,1,0:T(8,128)S(1)} %all-to-all-done.4.refs_0_), channel_id=1, source_target_pairs={{0,4},{4,0},{1,5},{5,1},{2,6},{6,2},{3,7},{7,3},{8,12},{12,8},{9,1... | collective-permute-start | bytes 3145736 | tf_op jit(solution)/shard_map/ppermute | solution.py:199
  257.2 69.3 %collective-permute-start.13 = (f32[4,32,16,128]{3,2,1,0:T(8,128)}, f32[4,32,16,128]{3,2,1,0:T(8,128)}, u32[]{:S(2)}, u32[]{:S(2)}) collective-permute-start(f32[4,32,16,128]{3,2,1,0:T(8,128)} %all-to-all-done.3.refs_0_), channel_id=1, source_target_pairs={{0,4},{4,0},{1,5},{5,1},{2,6},{6,2},{3,7},{7,3},{8,12},{12,8},{9,1... | collective-permute-start | bytes 3145736 | tf_op jit(solution)/shard_map/ppermute | solution.py:199
  258.6 25.2 %copy-start.2 = (f32[4,32,16,128]{3,2,1,0:T(8,128)}, f32[4,32,16,128]{3,2,1,0:T(8,128)S(1)}, u32[]{:S(2)}) copy-start(f32[4,32,16,128]{3,2,1,0:T(8,128)S(1)} %all-to-all-done.2.refs_0_) | copy-start | bytes 3145732
  258.6 89.7 %collective-permute-start.12 = (f32[4,32,16,128]{3,2,1,0:T(8,128)S(1)}, f32[4,32,16,128]{3,2,1,0:T(8,128)S(1)}, u32[]{:S(2)}, u32[]{:S(2)}) collective-permute-start(f32[4,32,16,128]{3,2,1,0:T(8,128)S(1)} %all-to-all-done.2.refs_0_), channel_id=1, source_target_pairs={{0,4},{4,0},{1,5},{5,1},{2,6},{6,2},{3,7},{7,3},{8,12},{12,8},{9,1... | collective-permute-start | bytes 3145736 | tf_op jit(solution)/shard_map/ppermute | solution.py:199
  283.8 1.0 copy-start.3
  348.3 1.0 copy-start.4
